TPU v7x, 128 devices: a whole 4x4x4 slice. The times are simulated.
128 devices in a mesh: seg: 4 (over x_hi, core), chan: 32 (over z, y, x_lo).
Axes of the slice: x: 4 (x_hi: 2, x_lo: 2; x = x_hi * 2 + x_lo), y: 4, z: 4, core: 2. Of those that a mesh axis runs over, the one named last changes fastest.
Arguments:
- traces: bfloat16 [32, 4096, 4096], P('seg', 'chan'), may hold values from -6 to 6
- channel_mask: int32 [4096], P('chan'), may hold values 0 or 1
- owner_ids: int32 [32, 64, 1], P('chan'), may hold values from 0 to 31; in each aligned block of 64 rows (0 to 63, 64 to 127, ..., all dimensions but the last counted through in order) at most 4 rows name the same one
- local_bins: int32 [32, 64], P('chan'), may hold values from 0 to 7
Outputs:
- stacks: float32 [256, 2048], P('chan')
Inputs may be any that keep to these rules, and one draw needn't show every extreme that they name: `owner_ids`: among the 64 tiles of one block no owner is named more than 4 times, a bound that some block reaches.
All inputs are finite; a program needn't handle non-finite values. No bound on the sum of `channel_mask` on one device may be relied on, other than what follows from the above.
Results may differ from a plain program's by a relative error of at most 0.0053.
Values may be sent and summed in bfloat16 or wider, within the bound.
A program may use at most 192 MiB of HBM per device.

v0:
```python
import math

import jax
import jax.numpy as jnp
from jax import lax
from jax.sharding import PartitionSpec as P

NT = 4096
DEC = 2
K0 = 8
HW = 64
R = 4
G = 16
BIN_DEV = 8
NB = 1024
NLAG = 2048


EPSILON = 1e-06


def passed_along(block, axis, distance):
    devices = range(lax.axis_size(axis))
    route = [(i - distance, i) for i in devices if i - distance in devices]
    return lax.ppermute(block, axis, route)


def forward_table():
    samples = jnp.arange(NT, dtype=jnp.int32)
    freqs = K0 + jnp.arange(NB, dtype=jnp.int32)
    phase = samples[:, None] * freqs[None, :] % NT
    angle = phase.astype(jnp.float32) * (2.0 * math.pi / NT)
    return jnp.concatenate([jnp.cos(angle), -jnp.sin(angle)], axis=1).astype(jnp.bfloat16)


def band_table():
    freqs = jnp.arange(NB, dtype=jnp.int32)
    return (jnp.abs(freqs[:, None] - freqs[None, :]) <= HW).astype(jnp.float32)


def inverse_rows(first_bin, bin_count):
    freqs = K0 + first_bin + jnp.arange(bin_count, dtype=jnp.int32)
    delays = (jnp.arange(NLAG, dtype=jnp.int32) - NLAG // 2) * DEC
    phase = jnp.mod(freqs[:, None] * delays[None, :], NT)
    angle = phase.astype(jnp.float32) * (2.0 * math.pi / NT)
    scale = 1.0 / math.sqrt(NB)
    return jnp.concatenate([jnp.cos(angle) * scale, -jnp.sin(angle) * scale], axis=0)


def inverse_table():
    return inverse_rows(0, NB)


def whiten(block, mask_float, table, band):
    segs, chans, length = block.shape
    spectrum = jnp.dot(
        block.reshape(segs * chans, length), table, preferred_element_type=jnp.float32
    )
    half = spectrum.shape[1] // 2
    real_part = spectrum[:, :half]
    imag_part = spectrum[:, half:]
    power = real_part * real_part + imag_part * imag_part
    counts = jnp.sum(band, axis=0)
    level = jnp.sqrt(jnp.dot(power, band, precision=lax.Precision.HIGHEST) / counts + EPSILON)
    weight = jnp.tile(mask_float, segs)[:, None] / level
    result = jnp.concatenate([real_part * weight, imag_part * weight], axis=1)
    return result.astype(jnp.bfloat16).reshape(segs, chans, 2 * half)


def cross(source, source_mask, target, target_mask, total_segs):
    half = source.shape[-1] // 2
    source_float = source.astype(jnp.float32)
    target_float = target.astype(jnp.float32)
    source_real = source_float[..., :half]
    source_imag = source_float[..., half:]
    target_real = target_float[..., :half]
    target_imag = target_float[..., half:]
    real_sum = jnp.sum(source_real * target_real + source_imag * target_imag, axis=0)
    imag_sum = jnp.sum(source_imag * target_real - source_real * target_imag, axis=0)
    chans = real_sum.shape[0]
    real_groups = real_sum.reshape(G, chans // G, half).sum(axis=1)
    imag_groups = imag_sum.reshape(G, chans // G, half).sum(axis=1)
    counts = (source_mask * target_mask).reshape(G, chans // G).sum(axis=1)
    scale = 1.0 / (total_segs * jnp.maximum(counts, 1.0))
    return jnp.concatenate([real_groups, imag_groups], axis=1) * scale[:, None]


def per_device(traces, channel_mask, owner_ids, local_bins):
    seg_count = lax.axis_size("seg")
    chan_count = lax.axis_size("chan")
    total_segs = traces.shape[0] * seg_count
    mask_float = channel_mask.astype(jnp.float32)
    whitened = whiten(traces, mask_float, forward_table(), band_table())
    mask_half = mask_float.astype(jnp.bfloat16)
    pieces = []
    for offset in range(1, R + 1):
        far_spectra, far_mask = passed_along((whitened, mask_half), "chan", -offset)
        pieces.append(
            cross(whitened, mask_float, far_spectra, far_mask.astype(jnp.float32), total_segs)
        )
    tiles = jnp.concatenate(pieces, axis=0)
    tiles = lax.psum(tiles, "seg")
    payload = jnp.dot(tiles, inverse_table(), precision=lax.Precision.HIGHEST)
    width = payload.shape[1]
    tile_count = payload.shape[0]
    capacity = 2 * tile_count // chan_count
    destination = owner_ids.reshape(-1)
    wanted_bins = local_bins.reshape(-1).astype(jnp.float32)
    onehot = (destination[:, None] == jnp.arange(chan_count, dtype=jnp.int32)[None, :]).astype(
        jnp.int32
    )
    earlier = jnp.cumsum(onehot, axis=0) - onehot
    slot_index = jnp.sum(earlier * onehot, axis=1)
    outgoing = (
        jnp.zeros((chan_count, capacity, width), jnp.float32)
        .at[destination, slot_index]
        .set(payload)
    )
    labels = (
        jnp.full((chan_count, capacity), -1.0, jnp.float32)
        .at[destination, slot_index]
        .set(wanted_bins)
    )
    arrived, arrived_labels = (
        lax.all_to_all(outgoing, "chan", split_axis=0, concat_axis=0, tiled=True),
        lax.all_to_all(labels, "chan", split_axis=0, concat_axis=0, tiled=True),
    )
    selector = (
        arrived_labels.reshape(1, -1) == jnp.arange(BIN_DEV, dtype=jnp.float32)[:, None]
    ).astype(jnp.float32)
    stacked = jnp.dot(selector, arrived.reshape(-1, width), precision=lax.Precision.HIGHEST)
    return stacked


def solution(mesh):
    in_specs = (P("seg", "chan", None), P("chan"), P("chan", None, None), P("chan", None))
    out_specs = P("chan", None)
    return jax.shard_map(
        per_device, mesh=mesh, in_specs=in_specs, out_specs=out_specs, check_vma=False
    )
```

profile of v0, /device:TPU:1, one launch (start us, length us, event | category | flops | bytes accessed | tf_op | source)
XLA Modules:
  0.0 658.3 jit_solution(15695276328399603658)
XLA Ops:
  6.5 0.2 convert_reduce_fusion
  6.8 67.5 %cosine_convert_fusion = (bf16[4096,1024]{1,0:T(8,128)(2,1)S(1)}, bf16[4096,1024]{1,0:T(8,128)(2,1)S(1)}) fusion(s32[1024]{0:T(1024)S(1)} %iota_add_fusion), kind=kLoop, calls=%fused_computation.17 | loop fusion | flops 71303168 | bytes 16781312 | tf_op jit(solution)/shard_map/convert.4
  74.3 22.2 %fusion.17 = f32[1024,2048]{1,0:T(8,128)} fusion(bf16[1024,4096]{1,0:T(8,128)(2,1)} %bitcast.45, bf16[4096,1024]{1,0:T(8,128)(2,1)S(1)} %get-tuple-element.28, bf16[4096,1024]{1,0:T(8,128)(2,1)S(1)} %get-tuple-element.27), kind=kOutput, calls=%fused_computation.31 | convolution fusion | flops 17213423616 | bytes 33554432 | tf_op jit(solution)/shard_map/dot_general | solution.py:56
  96.5 14.5 %multiply_convert_fusion.1 = (bf16[1024,1024]{1,0:T(8,128)(2,1)S(1)}, bf16[1024,1024]{1,0:T(8,128)(2,1)S(1)}) fusion(f32[1024,2048]{1,0:T(8,128)} %fusion.17, f32[1024]{0:T(1024)S(1)} %convert_reduce_fusion, f32[1024]{0:T(1024)S(1)} %broadcast_bitcast_fusion), kind=kOutput, calls=%fused_computation.42 | convolution fusion | flops 12898533376 | bytes 20979712 | tf_op jit(solution)/shard_map/dot_general | solution.py:64
  111.0 0.0 copy-start
  111.0 0.0 copy-start.2
  111.0 5.2 fusion.37
  116.3 1.3 collective-permute-start
  117.5 1.3 collective-permute-start.2
  118.8 1.3 collective-permute-start.4
  120.1 1.3 collective-permute-start.6
  121.4 1.3 collective-permute-start.1
  122.7 0.1 fusion.29
  122.8 0.1 reduce_window_sum.11
  122.9 0.2 select_reduce_fusion
  123.1 87.2 %collective-permute-done.1 = bf16[128]{0:T(256)(128)(2,1)S(1)} collective-permute-done((bf16[128]{0:T(256)(128)(2,1)S(1)}, bf16[128]{0:T(256)(128)(2,1)S(1)}, u32[]{:S(2)}, u32[]{:S(2)}) %collective-permute-start.1) | collective-permute-done | bytes 288 | tf_op jit(solution)/shard_map/ppermute | solution.py:25
  210.3 1.3 collective-permute-start.3
  211.6 93.1 %collective-permute-done.3 = bf16[128]{0:T(256)(128)(2,1)S(1)} collective-permute-done((bf16[128]{0:T(256)(128)(2,1)S(1)}, bf16[128]{0:T(256)(128)(2,1)S(1)}, u32[]{:S(2)}, u32[]{:S(2)}) %collective-permute-start.3) | collective-permute-done | bytes 288 | tf_op jit(solution)/shard_map/ppermute | solution.py:25
  304.7 1.3 collective-permute-start.5
  306.0 3.5 scatter_fusion
  309.5 0.7 copy.8
  310.2 189.5 %all-to-all-start = ((f32[32,1,4]{2,1,0:T(1,128)}), f32[32,1,4]{2,1,0:T(1,128)S(1)}, u32[]{:S(2)}, u32[]{:S(2)}) async-start(f32[32,1,4]{2,1,0:T(1,128)} %copy.8), calls=%async_computation | async-start | bytes 32768 | tf_op jit(solution)/shard_map/all_to_all | solution.py:126
  499.8 0.0 all-reduce.2.cloned.1.call-start
  499.8 0.0 collective-permute-done.5
  499.8 1.3 collective-permute-start.7
  501.1 4.5 collective-permute-done.7
  505.6 0.1 reshape.139
  505.7 0.1 reshape.142
  505.8 0.1 reduce_sum.207
  505.9 0.1 reduce_sum.212
  506.0 0.1 reshape.145
  506.1 0.1 reduce_sum.217
  506.3 0.1 reshape.148
  506.3 0.1 reduce_sum.222
  506.5 0.0 collective-permute-done
  506.5 6.5 convert_element_type.69
  513.0 6.5 convert_element_type.72
  519.5 0.0 collective-permute-done.4
  519.5 6.5 convert_element_type.74
  526.0 6.5 convert_element_type.76
  532.4 17.5 %add_reduce_fusion.3 = (f32[128,1024]{1,0:T(8,128)}, f32[128,1024]{1,0:T(8,128)}, f32[128,1024]{1,0:T(8,128)S(1)}, f32[128,1024]{1,0:T(8,128)S(1)}, f32[128,1024...) fusion(f32[8,128,2048]{2,1,0:T(8,128)} %convert_element_type.69, ...), kind=kLoop, calls=%fused_computation.40 | loop fusion | flops 32505856 | bytes 46137344 | tf_op jit(solution)/shard_map/reduce_sum | solution.py:78
  549.9 1.5 bitcast_reduce_fusion.6
  551.4 0.3 bitcast_reduce_fusion.4
  551.7 0.3 bitcast_reduce_fusion.2
  551.9 0.3 bitcast_reduce_fusion
  552.2 0.1 maximum_multiply_fusion
  552.3 0.1 maximum_multiply_fusion.1
  552.3 0.1 maximum_multiply_fusion.2
  552.4 0.1 maximum_multiply_fusion.3
  552.5 0.8 pad_maximum_fusion.1
  553.4 0.0 all-reduce.2.cloned.1.call-update
  553.4 35.6 %cosine_multiply_fusion = (f32[1024,2048]{1,0:T(8,128)}, f32[1024,2048]{1,0:T(8,128)}) fusion(s32[2048]{0:T(1024)S(1)} %add_multiply_fusion, s32[1024]{0:T(1024)S(1)} %iota_add_fusion), kind=kLoop, calls=%fused_computation.30 | loop fusion | flops 35651584 | bytes 16789504 | tf_op jit(solution)/shard_map/mul | solution.py:47
  589.0 10.6 %all-reduce.2.cloned.1.call-done = f32[64,2048]{1,0:T(8,128)} async-done(((f32[64,2048]{1,0:T(8,128)}), f32[64,2048]{1,0:T(8,128)}) %all-reduce.2.cloned.1.call-update) | async-done | bytes 524304 | tf_op jit(solution)/shard_map/psum | solution.py:102
  599.6 13.9 %fusion.7 = f32[64,2048]{1,0:T(8,128)S(1)} fusion(f32[64,2048]{1,0:T(8,128)} %all-reduce.2.cloned.1.call-done, f32[1024,2048]{1,0:T(8,128)} %get-tuple-element.26, f32[1024,2048]{1,0:T(8,128)} %get-tuple-element.25), kind=kOutput, calls=%fused_computation.12 | convolution fusion | flops 3225419776 | bytes 17825792 | tf_op jit(solution)/shard_map/dot_general | solution.py:103
  613.6 1.2 broadcast_in_dim.5
  614.8 11.0 %scatter_fusion.1 = f32[32,4,2048]{2,1,0:T(4,128)} fusion(f32[32,4,2048]{2,1,0:T(4,128)} %broadcast_in_dim.5, s32[64]{0:T(128)S(1)} %fusion.33, f32[64,2048]{1,0:T(8,128)S(1)} %fusion.7), kind=kCustom, calls=%fused_computation.1 | custom fusion | bytes 1573376 | tf_op jit(solution)/shard_map/scatter | solution.py:117
  625.8 0.0 all-to-all-done
  625.8 7.0 %all-to-all-start.1 = ((f32[32,4,2048]{2,1,0:T(4,128)}), f32[32,4,2048]{2,1,0:T(4,128)S(1)}, u32[]{:S(2)}, u32[]{:S(2)}) async-start(f32[32,4,2048]{2,1,0:T(4,128)} %scatter_fusion.1), calls=%async_computation.1 | async-start | bytes 2097152 | tf_op jit(solution)/shard_map/all_to_all | solution.py:125
  632.8 0.5 broadcast.209
  633.3 0.7 reduce.3
  634.0 0.1 eq.38
  634.1 15.9 %all-to-all-done.1 = f32[32,4,2048]{2,1,0:T(4,128)S(1)} async-done(((f32[32,4,2048]{2,1,0:T(4,128)}), f32[32,4,2048]{2,1,0:T(4,128)S(1)}, u32[]{:S(2)}, u32[]{:S(2)}) %all-to-all-start.1) | async-done | bytes 1048608 | tf_op jit(solution)/shard_map/all_to_all | solution.py:125
  650.0 0.4 reshape.149
  650.4 1.1 fusion.30
  (18 shorter events, 0.1 us)
Async XLA Ops:
  6.8 67.5 %copy-start.1 = (s32[128]{0:T(128)S(1)}, s32[128]{0:T(128)}, u32[]{:S(2)}) copy-start(s32[128]{0:T(128)} %param.5) | copy-start | bytes 1540
  111.0 11.7 %copy-start = (s32[1,64,1]{1,2,0:T(1,128)S(1)}, s32[1,64,1]{1,2,0:T(1,128)}, u32[]{:S(2)}) copy-start(s32[1,64,1]{1,2,0:T(1,128)} %param.6) | copy-start | bytes 772
  111.0 100.6 %copy-start.2 = (s32[1,64]{1,0:T(1,128)S(1)}, s32[1,64]{1,0:T(1,128)}, u32[]{:S(2)}) copy-start(s32[1,64]{1,0:T(1,128)} %param.7) | copy-start | bytes 772
  116.3 390.3 %collective-permute-start = (bf16[8,128,2048]{2,1,0:T(8,128)(2,1)}, bf16[8,128,2048]{2,1,0:T(8,128)(2,1)}, u32[]{:S(2)}, u32[]{:S(2)}) collective-permute-start(bf16[8,128,2048]{2,1,0:T(8,128)(2,1)} %get-tuple-element.24), channel_id=1, source_target_pairs={{1,0},{2,1},{3,2},{4,3},{5,4},{6,5},{7,6},{8,7},{9,8},{10,9},{11,1... | collective-permute-start | bytes 12582920 | tf_op jit(solution)/shard_map/ppermute | solution.py:25
  117.5 395.5 %collective-permute-start.2 = (bf16[8,128,2048]{2,1,0:T(8,128)(2,1)}, bf16[8,128,2048]{2,1,0:T(8,128)(2,1)}, u32[]{:S(2)}, u32[]{:S(2)}) collective-permute-start(bf16[8,128,2048]{2,1,0:T(8,128)(2,1)} %get-tuple-element.24), channel_id=1, source_target_pairs={{2,0},{3,1},{4,2},{5,3},{6,4},{7,5},{8,6},{9,7},{10,8},{11,9},{12,... | collective-permute-start | bytes 12582920 | tf_op jit(solution)/shard_map/ppermute | solution.py:25
  118.8 400.6 %collective-permute-start.4 = (bf16[8,128,2048]{2,1,0:T(8,128)(2,1)}, bf16[8,128,2048]{2,1,0:T(8,128)(2,1)}, u32[]{:S(2)}, u32[]{:S(2)}) collective-permute-start(bf16[8,128,2048]{2,1,0:T(8,128)(2,1)} %get-tuple-element.24), channel_id=1, source_target_pairs={{3,0},{4,1},{5,2},{6,3},{7,4},{8,5},{9,6},{10,7},{11,8},{12,9},{13... | collective-permute-start | bytes 12582920 | tf_op jit(solution)/shard_map/ppermute | solution.py:25
  120.1 405.8 %collective-permute-start.6 = (bf16[8,128,2048]{2,1,0:T(8,128)(2,1)}, bf16[8,128,2048]{2,1,0:T(8,128)(2,1)}, u32[]{:S(2)}, u32[]{:S(2)}) collective-permute-start(bf16[8,128,2048]{2,1,0:T(8,128)(2,1)} %get-tuple-element.24), channel_id=1, source_target_pairs={{4,0},{5,1},{6,2},{7,3},{8,4},{9,5},{10,6},{11,7},{12,8},{13,9},{1... | collective-permute-start | bytes 12582920 | tf_op jit(solution)/shard_map/ppermute | solution.py:25
  121.4 88.9 %collective-permute-start.1 = (bf16[128]{0:T(256)(128)(2,1)S(1)}, bf16[128]{0:T(256)(128)(2,1)S(1)}, u32[]{:S(2)}, u32[]{:S(2)}) collective-permute-start(bf16[128]{0:T(256)(128)(2,1)S(1)} %get-tuple-element.33), channel_id=1, source_target_pairs={{1,0},{2,1},{3,2},{4,3},{5,4},{6,5},{7,6},{8,7},{9,8},{10,9},{11,1... | collective-permute-start | bytes 776 | tf_op jit(solution)/shard_map/ppermute | solution.py:25
  210.3 94.4 %collective-permute-start.3 = (bf16[128]{0:T(256)(128)(2,1)S(1)}, bf16[128]{0:T(256)(128)(2,1)S(1)}, u32[]{:S(2)}, u32[]{:S(2)}) collective-permute-start(bf16[128]{0:T(256)(128)(2,1)S(1)} %get-tuple-element.33), channel_id=1, source_target_pairs={{2,0},{3,1},{4,2},{5,3},{6,4},{7,5},{8,6},{9,7},{10,8},{11,9},{12,... | collective-permute-start | bytes 776 | tf_op jit(solution)/shard_map/ppermute | solution.py:25
  304.7 195.1 %collective-permute-start.5 = (bf16[128]{0:T(256)(128)(2,1)S(1)}, bf16[128]{0:T(256)(128)(2,1)S(1)}, u32[]{:S(2)}, u32[]{:S(2)}) collective-permute-start(bf16[128]{0:T(256)(128)(2,1)S(1)} %get-tuple-element.33), channel_id=1, source_target_pairs={{3,0},{4,1},{5,2},{6,3},{7,4},{8,5},{9,6},{10,7},{11,8},{12,9},{13... | collective-permute-start | bytes 776 | tf_op jit(solution)/shard_map/ppermute | solution.py:25
  310.2 315.6 %all-to-all-start = ((f32[32,1,4]{2,1,0:T(1,128)}), f32[32,1,4]{2,1,0:T(1,128)S(1)}, u32[]{:S(2)}, u32[]{:S(2)}) async-start(f32[32,1,4]{2,1,0:T(1,128)} %copy.8), calls=%async_computation | async-start | bytes 32768 | tf_op jit(solution)/shard_map/all_to_all | solution.py:126
  499.8 99.8 %all-reduce.2.cloned.1.call-start = ((), (), s32[]{:S(2)}) async-start(), calls=%async_computation.2 | async-start | bytes 1048576 | tf_op jit(solution)/shard_map/psum | solution.py:102
  499.8 5.8 collective-permute-start.7
  625.8 24.2 %all-to-all-start.1 = ((f32[32,4,2048]{2,1,0:T(4,128)}), f32[32,4,2048]{2,1,0:T(4,128)S(1)}, u32[]{:S(2)}, u32[]{:S(2)}) async-start(f32[32,4,2048]{2,1,0:T(4,128)} %scatter_fusion.1), calls=%async_computation.1 | async-start | bytes 2097152 | tf_op jit(solution)/shard_map/all_to_all | solution.py:125
Sparse Core Ops, SparseCore 0:
  553.5 46.0 all-reduce.1
where the time goes:
time: 659 us; the launch traced here: 658 us
  waiting for transfers between devices  211 us (32%)
  starting transfers between devices  207 us (31%)
  other arithmetic  157 us (24%)
  matrix products  51.7 us (8%)
  local copies, waits for them, and re-layouts  17.8 us (3%)
  between operations  13.7 us (2%)
    all_to_all x1, starting transfers between devices, per_device(): lax.all_to_all(labels, 'chan', split_axis=0, concat_axis=0, tiled=True)  190 us
    ppermute x8, waiting for transfers between devices, passed_along(): return lax.ppermute(block, axis, route)  185 us
    another operation x1, other arithmetic  67.5 us
    mul x1, other arithmetic, inverse_rows(): jnp.cos(angle) * scale  35.6 us
    convert_element_type x4, other arithmetic, cross(): target_float = target.astype(jnp.float32)  25.9 us
    dot_general x1, matrix products, whiten(): jnp.dot(block.reshape(segs * chans, length), table, preferred_element_typ...  22.2 us
    reduce_sum x1, other arithmetic, cross(): jnp.sum(source_real * target_real + source_imag * target_imag, axis=0)  17.5 us
    all_to_all x1, waiting for transfers between devices, per_device(): lax.all_to_all(outgoing, 'chan', split_axis=0, concat_axis=0, tiled=True)  15.9 us
  transfers between devices with their start and end apart: 11, of which 5 were waited for; matrix products, arithmetic and copies ran while one was open for 18% of the time, Pallas kernels for 0%

commit v1 on v0

v1 whole, which is shorter than its diff:
```python
import functools
import math

import jax
import jax.numpy as jnp
import numpy as np
from jax import lax
from jax.experimental import pallas as pl
from jax.experimental.pallas import tpu as pltpu
from jax.sharding import PartitionSpec as P

CB = 128
NT = 4096
K0 = 8
HW = 64
R = 4
G = 16
BIN_DEV = 8
NB = 1024
NLAG = 2048
HALF = NB // 2
EPSILON = 1e-06
STEPS = 4
MESH = pl.DeviceIdType.MESH


def small_tables():
    freqs = K0 + np.arange(NB)
    coarse = (np.arange(16)[:, None, None] * 64 * freqs[None, None, :]) % NT * (2.0 * math.pi / NT)
    fine = (np.arange(64)[:, None] * freqs[None, :]) % NT * (2.0 * math.pi / NT)
    return [
        jnp.asarray(t, jnp.float32)
        for t in (np.cos(coarse), -np.sin(coarse), np.cos(fine), -np.sin(fine))
    ]


def peer(c, r):
    x, y, z = c % 2, (c // 2) % 4, c // 8
    return ((z + r % 4) % 4) * 8 + ((y + (r // 4) % 4) % 4) * 2 + (x + r // 16) % 2


def spectra_kernel(
    traces, coarse_re, coarse_im, fine_re, fine_im, mask_ref,
    out_ref,
    x_ref, tab, spec, power, inv_level, send, recv, acc,
    x_sem, own_sem, send_sem, recv_sem,
):
    chans = lax.axis_size("chan")
    me = lax.axis_index("chan")
    segs = 8 // STEPS
    rows = segs * CB

    def load(i):
        part = pl.ds(i * segs, segs)
        return pltpu.make_async_copy(traces.at[part], x_ref.at[part], x_sem.at[i])

    for i in range(STEPS):
        load(i).start()

    barrier = pltpu.get_barrier_semaphore()

    def greet(r, carry):
        pl.semaphore_signal(barrier, inc=1, device_id={"chan": peer(me, r)}, device_id_type=MESH)
        return carry

    lax.fori_loop(1, chans, greet, 0)

    turn = lax.broadcasted_iota(jnp.int32, (64, 128), 1) % 4
    c0 = jnp.where(turn == 0, 1.0, jnp.where(turn == 2, -1.0, 0.0)).astype(jnp.bfloat16)
    c1 = jnp.where(turn == 1, 1.0, jnp.where(turn == 3, -1.0, 0.0)).astype(jnp.bfloat16)
    flip = jnp.where(turn % 2 == 0, 1.0, -1.0).astype(jnp.bfloat16)

    def make_rows(a, carry):
        for chunk in range(NB // 128):
            cols = pl.ds(chunk * 128, 128)
            ar, ai = coarse_re[a, :, cols], coarse_im[a, :, cols]
            br, bi = fine_re[:, cols], fine_im[:, cols]
            re = (ar * br - ai * bi).astype(jnp.bfloat16)
            im = (ar * bi + ai * br).astype(jnp.bfloat16)
            re1, im1 = re * c0 + im * c1, im * c0 - re * c1
            base = (chunk // 4) * NB + (chunk % 4) * 128
            for quarter, (u, v) in enumerate(
                ((re, im), (re1, im1), (re * flip, im * flip), (re1 * flip, im1 * flip))
            ):
                at = pl.ds(pl.multiple_of(quarter * 1024 + a * 64, 64), 64)
                tab[at, pl.ds(base, 128)] = u
                tab[at, pl.ds(base + HALF, 128)] = v
        return carry

    lax.fori_loop(0, 16, make_rows, 0)

    power[:, pl.ds(0, 128)] = jnp.zeros((rows, 128), jnp.bfloat16)
    power[:, pl.ds(128 + NB, 128)] = jnp.zeros((rows, 128), jnp.bfloat16)
    recv[:, pl.ds(chans, R)] = jnp.zeros((STEPS, R, 8 * segs, NB), jnp.bfloat16)
    near = (
        lax.broadcasted_iota(jnp.int32, (512, 256), 0)
        - lax.broadcasted_iota(jnp.int32, (512, 256), 1)
        - 128
    )
    band = jnp.where(jnp.abs(near) <= HW, 1.0, 0.0).astype(jnp.bfloat16)
    pl.semaphore_wait(barrier, chans - 1)

    def exchange(i, r):
        to = peer(me, r)
        return pltpu.make_async_remote_copy(
            send.at[i, to // 2, to % 2],
            recv.at[i, me],
            send_sem.at[i, to],
            recv_sem.at[i, me],
            device_id={"chan": to},
            device_id_type=MESH,
        )

    def arrival(i, r):
        source = peer(me, r)
        return pltpu.make_async_copy(recv.at[i, source], recv.at[i, source], recv_sem.at[i, source])

    def keep(i):
        return pltpu.make_async_copy(send.at[i, me // 2, me % 2], recv.at[i, me], own_sem.at[i])

    def whiten_step(i, carry):
        load(i).wait()

        def transform(n, carry):
            cols = pl.ds(pl.multiple_of(n * 256, 256), 256)
            block = x_ref[pl.ds(i * segs, segs)].reshape(rows, NT)
            spec[:, cols] = jnp.dot(block, tab[:, cols], preferred_element_type=jnp.float32)
            return carry

        lax.fori_loop(0, 2 * NB // 256, transform, 0)

        def add_power(n, carry):
            at = pl.ds(pl.multiple_of(n * 32, 32), 32)
            for chunk in range(NB // 256):
                base = (chunk // 2) * NB + (chunk % 2) * 256
                re, im = spec[at, pl.ds(base, 256)], spec[at, pl.ds(base + HALF, 256)]
                power[at, pl.ds(128 + chunk * 256, 256)] = (re * re + im * im).astype(jnp.bfloat16)
            return carry

        lax.fori_loop(0, rows // 32, add_power, 0)

        for chunk in range(NB // 256):
            total = jnp.dot(
                power[:, pl.ds(chunk * 256, 512)], band, preferred_element_type=jnp.float32
            )
            k = chunk * 256 + lax.broadcasted_iota(jnp.int32, (1, 256), 1)
            count = jnp.minimum(k + HW, NB - 1) - jnp.maximum(k - HW, 0) + 1
            inv_level[:, pl.ds(chunk * 256, 256)] = lax.rsqrt(
                total * (1.0 / count.astype(jnp.float32)) + EPSILON
            )

        def scale(g, carry):
            valid = mask_ref[pl.ds(pl.multiple_of(g * 8, 8), 8), :]
            for chunk in range(NB // 128):
                h, at = chunk // 4, (chunk % 4) * 128
                res, ims = [], []
                for s in range(segs):
                    row = pl.ds(pl.multiple_of(s * CB + g * 8, 8), 8)
                    weight = inv_level[row, pl.ds(chunk * 128, 128)] * valid
                    res.append(spec[row, pl.ds(h * NB + at, 128)] * weight)
                    ims.append(spec[row, pl.ds(h * NB + HALF + at, 128)] * weight)
                send[i, g, h, :, pl.ds(at, 128)] = jnp.concatenate(res, 0).astype(jnp.bfloat16)
                send[i, g, h, :, pl.ds(HALF + at, 128)] = jnp.concatenate(ims, 0).astype(jnp.bfloat16)
            return carry

        lax.fori_loop(0, G, scale, 0)

        def start(r, carry):
            exchange(i, r).start()
            return carry

        keep(i).start()
        lax.fori_loop(1, chans, start, 0)
        return carry

    lax.fori_loop(0, STEPS, whiten_step, 0)

    acc[...] = jnp.zeros_like(acc)

    def cross_step(i, carry):
        def take(r, carry):
            arrival(i, r).wait()
            return carry

        lax.fori_loop(1, chans, take, 0)
        keep(i).wait()

        def products(n, carry):
            chunk = n % 4
            first = (n // 4) * 4
            re_at = pl.ds(pl.multiple_of(chunk * 128, 128), 128)
            im_at = pl.ds(pl.multiple_of(HALF + chunk * 128, 128), 128)
            re = [recv[i, first + j, :, re_at].astype(jnp.float32) for j in range(4 + R)]
            im = [recv[i, first + j, :, im_at].astype(jnp.float32) for j in range(4 + R)]
            for j in range(4):
                for d in range(1, R + 1):
                    p = re[j] * re[j + d] + im[j] * im[j + d]
                    q = im[j] * re[j + d] - re[j] * im[j + d]
                    t = (first + j) * R + d - 1
                    acc[chunk, t, :, pl.ds(0, 128)] += p.reshape(segs, 8, 128).sum(0)
                    acc[chunk, t, :, pl.ds(128, 128)] += q.reshape(segs, 8, 128).sum(0)
            return carry

        lax.fori_loop(0, chans, products, 0)
        return carry

    lax.fori_loop(0, STEPS, cross_step, 0)

    def reduce_rows(n, carry):
        at = pl.ds(pl.multiple_of((n // 4) * 8, 8), 8)
        out_ref[n % 4, at, :] = acc[n % 4, at].sum(1)
        return carry

    lax.fori_loop(0, 4 * chans * R // 8, reduce_rows, 0)

    def finish(n, carry):
        exchange(n // chans, n % chans).wait_send()
        return carry

    for i in range(STEPS):
        lax.fori_loop(i * chans + 1, (i + 1) * chans, finish, 0)


def tile_sums(traces, mask_float):
    chans = lax.axis_size("chan")
    tiles = chans * R
    segs = traces.shape[0] // STEPS
    vmem = pl.BlockSpec(memory_space=pltpu.VMEM)
    return pl.pallas_call(
        spectra_kernel,
        out_shape=jax.ShapeDtypeStruct((4, tiles, 256), jnp.float32),
        in_specs=[pl.BlockSpec(memory_space=pl.ANY)] + [vmem] * 5,
        out_specs=vmem,
        scratch_shapes=[
            pltpu.VMEM(traces.shape, jnp.bfloat16),
            pltpu.VMEM((NT, 2 * NB), jnp.bfloat16),
            pltpu.VMEM((segs * CB, 2 * NB), jnp.float32),
            pltpu.VMEM((segs * CB, NB + 256), jnp.bfloat16),
            pltpu.VMEM((segs * CB, NB), jnp.float32),
            pltpu.VMEM((STEPS, G, 2, 8 * segs, NB), jnp.bfloat16),
            pltpu.VMEM((STEPS, chans + R, 8 * segs, NB), jnp.bfloat16),
            pltpu.VMEM((4, tiles, 8, 256), jnp.float32),
            pltpu.SemaphoreType.DMA((STEPS,)),
            pltpu.SemaphoreType.DMA((STEPS,)),
            pltpu.SemaphoreType.DMA((STEPS, chans)),
            pltpu.SemaphoreType.DMA((STEPS, chans)),
        ],
        compiler_params=pltpu.CompilerParams(
            collective_id=0, has_side_effects=True, vmem_limit_bytes=56 << 20
        ),
        name="spectra",
    )(traces, *small_tables(), jnp.broadcast_to(mask_float[:, None], (CB, 128)))


def inverse_rows(first_bin):
    freqs = K0 + first_bin + jnp.arange(128, dtype=jnp.int32)
    unit = 2.0 * math.pi / NT
    a = jnp.mod(freqs[:, None] * (jnp.arange(16, dtype=jnp.int32) * 128 - NLAG // 2)[None, :] * 2, NT)
    b = jnp.mod(freqs[:, None] * jnp.arange(128, dtype=jnp.int32)[None, :] * 2, NT)
    a, b = a.astype(jnp.float32) * unit, b.astype(jnp.float32) * unit
    scale = 1.0 / math.sqrt(NB)
    ca, sa = (jnp.cos(a) * scale)[:, :, None], (jnp.sin(a) * scale)[:, :, None]
    cb, sb = jnp.cos(b)[:, None, :], jnp.sin(b)[:, None, :]
    cos = (ca * cb - sa * sb).reshape(128, NLAG)
    sin = (sa * cb + ca * sb).reshape(128, NLAG)
    return jnp.concatenate([cos, -sin], axis=0)


def per_device(traces, channel_mask, owner_ids, local_bins):
    seg_count = lax.axis_size("seg")
    chan_count = lax.axis_size("chan")
    total_segs = traces.shape[0] * seg_count
    me = lax.axis_index("chan")
    group = me // 2
    labels = owner_ids.reshape(-1) * BIN_DEV + local_bins.reshape(-1)
    every = lax.all_gather(jnp.concatenate([channel_mask, labels]), "chan")
    masks = lax.dynamic_slice_in_dim(every[:, :CB].reshape(chan_count, G, 8), group, 1, 1)[:, 0]
    masks = jnp.pad(masks.astype(jnp.float32), ((0, R), (0, 0)))
    labels = lax.dynamic_slice_in_dim(every[:, CB:].reshape(chan_count, R, G), group, 1, 2)[..., 0]
    counts = jnp.stack(
        [(masks[:chan_count] * masks[d : d + chan_count]).sum(1) for d in range(1, R + 1)], 1
    )
    scale = 1.0 / (total_segs * jnp.maximum(counts, 1.0))
    bins = jnp.arange(chan_count * BIN_DEV, dtype=jnp.int32)
    stacker = jnp.where(bins[:, None] == labels.reshape(1, -1), scale.reshape(1, -1), 0.0)

    raw = tile_sums(traces, channel_mask.astype(jnp.float32))
    sums = lax.psum_scatter(raw, "seg", scatter_dimension=0, tiled=False)
    stacked = jnp.dot(stacker, sums, precision=lax.Precision.HIGHEST)
    arrived = lax.all_to_all(
        stacked.reshape(chan_count, BIN_DEV, 256), "chan", split_axis=0, concat_axis=0, tiled=True
    )
    spectra = arrived.reshape(G, 2, BIN_DEV, 256).sum(0)
    first = lax.axis_index("seg") * 128
    lags = jnp.dot(spectra[0], inverse_rows(first), precision=lax.Precision.HIGHEST)
    lags += jnp.dot(spectra[1], inverse_rows(first + HALF), precision=lax.Precision.HIGHEST)
    return lax.psum(lags, "seg")


def solution(mesh):
    in_specs = (P("seg", "chan", None), P("chan"), P("chan", None, None), P("chan", None))
    return jax.shard_map(
        per_device, mesh=mesh, in_specs=in_specs, out_specs=P("chan", None), check_vma=False
    )
```

time: 659 us -> 311 us (0.47)
  starting transfers between devices: 207 us -> 3.91 us
  other arithmetic: 157 us -> 2.99 us
  waiting for transfers between devices: 211 us -> 74 us
  blocking collectives: 0 us -> 127 us
  Pallas kernels: 0 us -> 77.1 us
  matrix products: 51.7 us -> 4.86 us
  local copies, waits for them, and re-layouts: 17.8 us -> 6.33 us
    all_to_all x2 -> x1, starting transfers between devices: 197 us -> 3.87 us  [per_device(): lax.all_to_all(stacked.reshape(chan_count, BIN_DEV, 256), 'chan', split_a...]
    ppermute x8 -> x0, waiting for transfers between devices: 185 us -> none  [passed_along(): return lax.ppermute(block, axis, route)]
    unnamed x0 -> x1, blocking collectives: none -> 127 us
    pallas_call x0 -> x1, Pallas kernels: none -> 77.1 us  [tile_sums(): pl.pallas_call(spectra_kernel, out_shape=jax.ShapeDtypeStruct((4, tiles,...]
    another operation x2 -> x0, other arithmetic: 67.6 us -> none
    psum x1, waiting for transfers between devices: 10.6 us -> 68 us  [per_device(): return lax.psum(lags, 'seg')]
    dot_general x4 -> x3, matrix products: 51.7 us -> 4.86 us  [the longest x1 2.04 us: per_device(): stacked = jnp.dot(stacker, sums, precision=lax.Precision.HIGHEST)]
    mul x7 -> x1, other arithmetic: 36 us -> 0.16 us  [inverse_rows(): jnp.cos(a) * scale]
  transfers between devices with their start and end apart: 11 -> 3, of which waited for: 5 -> 2; matrix products, arithmetic and copies ran while one was open for 18% -> 2% of each run, Pallas kernels for 0% -> 0%
where the time goes in v1:
time: 311 us
  blocking collectives  127 us (41%)
  Pallas kernels  77.1 us (25%)
  waiting for transfers between devices  74 us (24%)
  between operations  14.3 us (5%)
  local copies, waits for them, and re-layouts  6.33 us (2%)
  matrix products  4.86 us (2%)
  starting transfers between devices  3.91 us (1%)
    unnamed x1, blocking collectives  127 us
    pallas_call x1, Pallas kernels, tile_sums(): pl.pallas_call(spectra_kernel, out_shape=jax.ShapeDtypeStruct((4, tiles,...  77.1 us
    psum x1, waiting for transfers between devices, per_device(): return lax.psum(lags, 'seg')  68 us
  transfers between devices with their start and end apart: 3, of which 2 were waited for; matrix products, arithmetic and copies ran while one was open for 2% of the time, Pallas kernels for 0%

profile of v1, /device:TPU:1, one launch (start us, length us, event | category | flops | bytes accessed | tf_op | source)
XLA Modules:
  0.0 310.7 jit_solution(15856138465626100802)
XLA Ops:
  6.5 0.0 reduce-scatter.2.cloned.1.call-start
  6.5 0.7 convert_element_type.53
  7.2 0.7 broadcast_in_dim.16.mask_ref
  7.9 0.0 copy-start.4
  7.9 0.0 copy-start.2
  7.9 0.0 copy-start.3
  7.9 0.0 copy-start.1
  7.9 77.1 %spectra.1 = f32[4,128,256]{2,1,0:T(8,128)} custom-call(bf16[8,128,4096]{2,1,0:T(8,128)(2,1)} %traces.1, f32[16,1,1024]{2,1,0:T(1,128)} %constant.94.clone.coarse_re, f32[16,1,1024]{2,1,0:T(1,128)} %constant.95.clone.coarse_im, f32[64,1024]{1,0:T(8,128)} %constant.96.clone.fine_re, f32[64,1024]{1,0:T(8,128)} %constant.97.clone.fine_im, ...), custom_call_target="tpu_custom_call" | custom-call | tf_op jit(solution)/shard_map/spectra/pallas_call | solution.py:229
  85.1 0.0 reduce-scatter.2.cloned.1.call-update
  85.1 0.0 copy-done.4
  85.1 0.6 dynamic-slice
  86.3 0.0 copy-done.2
  86.3 0.0 copy-done.3
  86.4 0.0 copy-done.1
  86.4 0.1 add_dynamic-update-slice_fusion
  86.5 127.3 %all-reduce.1 = s32[6144]{0:T(1024)S(1)} all-reduce(s32[6144]{0:T(1024)S(1)} %add_dynamic-update-slice_fusion), channel_id=2, replica_groups=mesh['seg'=4,'chan'=32] {'chan'}, use_global_device_ids=true, to_apply=%add.1 | all-reduce | flops 6144 | bytes 49152
  213.8 0.1 reshape.346
  213.9 0.1 copy.18
  214.0 0.1 multiply_reduce_fusion.3
  214.1 0.1 copy.19
  214.2 0.1 div.22
  214.3 0.1 copy.16
  214.4 0.1 copy.17
  214.5 0.1 eq.36
  214.7 0.2 cosine_multiply_fusion
  214.8 0.1 copy.20
  214.9 0.1 copy.21
  215.0 0.3 fusion.24
  215.4 0.6 multiply_subtract_fusion.1
  216.0 0.3 copy.34
  216.3 0.3 copy.35
  216.7 0.1 copy.22
  216.8 0.1 copy.23
  216.9 0.3 fusion.22
  217.2 0.0 reduce-scatter.2.cloned.1.call-done
  217.3 2.0 fusion.7
  219.3 3.9 %all-to-all-start = ((f32[32,8,256]{2,1,0:T(8,128)}), f32[32,8,256]{2,1,0:T(8,128)S(1)}, u32[]{:S(2)}, u32[]{:S(2)}) async-start(f32[32,8,256]{2,1,0:T(8,128)} %fusion.7), calls=%async_computation.1 | async-start | bytes 524288 | tf_op jit(solution)/shard_map/all_to_all | solution.py:290
  223.2 0.0 all-reduce.4.cloned.1.call-start
  223.2 0.6 multiply_subtract_fusion
  223.8 0.3 copy.32
  224.2 1.3 copy.33
  225.5 5.9 %all-to-all-done = f32[32,8,256]{2,1,0:T(8,128)S(1)} async-done(((f32[32,8,256]{2,1,0:T(8,128)}), f32[32,8,256]{2,1,0:T(8,128)S(1)}, u32[]{:S(2)}, u32[]{:S(2)}) %all-to-all-start) | async-done | bytes 262176 | tf_op jit(solution)/shard_map/all_to_all | solution.py:290
  231.5 0.0 copy-start
  231.5 1.1 fusion
  232.6 0.1 copy-done
  232.7 1.7 convolution_add_fusion
  234.4 0.0 all-reduce.4.cloned.1.call-update
  234.5 68.0 %all-reduce.4.cloned.1.call-done = f32[8,2048]{1,0:T(8,128)} async-done(((f32[8,2048]{1,0:T(8,128)}), f32[8,2048]{1,0:T(8,128)}) %all-reduce.4.cloned.1.call-update) | async-done | bytes 65552 | tf_op jit(solution)/shard_map/psum | solution.py:297
  302.4 1.5 copy.38
  (11 shorter events, 0.1 us)
Async XLA Ops:
  6.5 210.7 %reduce-scatter.2.cloned.1.call-start = ((), (), s32[]{:S(2)}) async-start(), calls=%async_computation.2 | async-start | bytes 655360 | tf_op jit(solution)/shard_map/reduce_scatter | solution.py:288
  7.9 77.2 %copy-start.4 = (u32[128]{0:T(128)S(1)}, u32[128]{0:T(128)}, u32[]{:S(2)}) copy-start(u32[128]{0:T(128)} %constant.104) | copy-start | bytes 1540
  7.9 78.4 %copy-start.2 = (s32[1,64]{1,0:T(1,128)S(1)}, s32[1,64]{1,0:T(1,128)}, u32[]{:S(2)}) copy-start(s32[1,64]{1,0:T(1,128)} %param.11) | copy-start | bytes 772
  7.9 78.4 %copy-start.3 = (s32[1,64,1]{1,2,0:T(1,128)S(1)}, s32[1,64,1]{1,2,0:T(1,128)}, u32[]{:S(2)}) copy-start(s32[1,64,1]{1,2,0:T(1,128)} %param.10) | copy-start | bytes 772
  7.9 78.5 %copy-start.1 = (s32[128]{0:T(128)S(1)}, s32[128]{0:T(128)}, u32[]{:S(2)}) copy-start(s32[128]{0:T(128)} %param.9) | copy-start | bytes 1540
  219.3 12.2 %all-to-all-start = ((f32[32,8,256]{2,1,0:T(8,128)}), f32[32,8,256]{2,1,0:T(8,128)S(1)}, u32[]{:S(2)}, u32[]{:S(2)}) async-start(f32[32,8,256]{2,1,0:T(8,128)} %fusion.7), calls=%async_computation.1 | async-start | bytes 524288 | tf_op jit(solution)/shard_map/all_to_all | solution.py:290
  223.2 79.2 %all-reduce.4.cloned.1.call-start = ((), (), s32[]{:S(2)}) async-start(), calls=%async_computation.3 | async-start | bytes 131072 | tf_op jit(solution)/shard_map/psum | solution.py:297
  231.5 1.2 copy-start
Sparse Core Ops, SparseCore 0:
  85.2 29.3 reduce-scatter.1
  234.6 67.7 all-reduce.3

commit v2 on v1

v2 whole, which is shorter than its diff:
```python
import functools
import math

import jax
import jax.numpy as jnp
import numpy as np
from jax import lax
from jax.experimental import pallas as pl
from jax.experimental.pallas import tpu as pltpu
from jax.sharding import PartitionSpec as P

CB = 128
NT = 4096
K0 = 8
HW = 64
R = 4
G = 16
BIN_DEV = 8
NB = 1024
NLAG = 2048
HALF = NB // 2
EPSILON = 1e-06
STEPS = 4
MESH = pl.DeviceIdType.MESH


def forward_factors():
    freqs = K0 + np.arange(NB)
    unit = 2.0 * math.pi / NT
    coarse = (np.arange(16)[:, None, None] * 64 * freqs[None, None, :]) % NT * unit
    fine = (np.arange(64)[:, None] * freqs[None, :]) % NT * unit
    tables = (np.cos(coarse), -np.sin(coarse), np.cos(fine), -np.sin(fine))
    return [jnp.asarray(t, jnp.float32) for t in tables]


def inverse_factors():
    unit = 2.0 * math.pi / NT
    freqs = K0 + np.arange(NB)
    fine = (freqs[:, None] * np.arange(128)[None, :] * 2) % NT * unit
    coarse = (freqs[None, :16] * (np.arange(16)[:, None] * 128 - NLAG // 2) * 2) % NT * unit
    fine = np.stack([np.cos(fine), np.sin(fine)]).reshape(2, 2, 4, 128, 128)
    coarse = np.stack([np.cos(coarse), np.sin(coarse)]) / math.sqrt(NB)
    coarse = np.broadcast_to(coarse[..., None], (2, 16, 16, 128))
    return [jnp.asarray(fine, jnp.float32), jnp.asarray(coarse, jnp.float32)]


def peer(c, r):
    x, y, z = c % 2, (c // 2) % 4, c // 8
    return ((z + r % 4) % 4) * 8 + ((y + (r // 4) % 4) % 4) * 2 + (x + r // 16) % 2


def loop(first, last, body):
    def step(n, carry):
        body(n)
        return carry

    lax.fori_loop(first, last, step, 0)


def stack_kernel(
    total_segs,
    traces, coarse_re, coarse_im, fine_re, fine_im, inv_fine, inv_coarse, info_ref,
    out_ref,
    x_ref, tab, spec, power, inv_level, valid_ref, send, recv, acc,
    fine_ref, inv_hi, inv_lo, info, onehot, scale_ref, raw, raw_in, bins, bins_in, part, part_in,
    x_sem, fine_sem, own_sem, send_sem, recv_sem,
    info_send, info_recv, raw_send, raw_recv, bins_send, bins_recv, part_send, part_recv,
):
    chans = lax.axis_size("chan")
    quarters = lax.axis_size("seg")
    me = lax.axis_index("chan")
    seg = lax.axis_index("seg")
    segs = x_ref.shape[0] // STEPS
    rows = segs * CB
    tiles = chans * R

    def load(i):
        part_of = pl.ds(i * segs, segs)
        return pltpu.make_async_copy(traces.at[part_of], x_ref.at[part_of], x_sem.at[i])

    def load_fine():
        return pltpu.make_async_copy(inv_fine.at[:, :, seg], fine_ref, fine_sem)

    for i in range(STEPS):
        load(i).start()
    load_fine().start()

    barrier = pltpu.get_barrier_semaphore()

    def greet(r):
        pl.semaphore_signal(barrier, inc=1, device_id={"chan": peer(me, r)}, device_id_type=MESH)

    def greet_seg(q):
        to = (seg + q) % quarters
        pl.semaphore_signal(barrier, inc=1, device_id={"seg": to}, device_id_type=MESH)

    loop(1, chans, greet)
    loop(1, quarters, greet_seg)

    turn = lax.broadcasted_iota(jnp.int32, (64, 128), 1) % 4
    c0 = jnp.where(turn == 0, 1.0, jnp.where(turn == 2, -1.0, 0.0)).astype(jnp.bfloat16)
    c1 = jnp.where(turn == 1, 1.0, jnp.where(turn == 3, -1.0, 0.0)).astype(jnp.bfloat16)
    flip = jnp.where(turn % 2 == 0, 1.0, -1.0).astype(jnp.bfloat16)

    def make_rows(a):
        for chunk in range(NB // 128):
            cols = pl.ds(chunk * 128, 128)
            ar, ai = coarse_re[a, :, cols], coarse_im[a, :, cols]
            br, bi = fine_re[:, cols], fine_im[:, cols]
            re = (ar * br - ai * bi).astype(jnp.bfloat16)
            im = (ar * bi + ai * br).astype(jnp.bfloat16)
            re1, im1 = re * c0 + im * c1, im * c0 - re * c1
            base = (chunk // 4) * NB + (chunk % 4) * 128
            for quarter, (u, v) in enumerate(
                ((re, im), (re1, im1), (re * flip, im * flip), (re1 * flip, im1 * flip))
            ):
                at = pl.ds(pl.multiple_of(quarter * 1024 + a * 64, 64), 64)
                tab[at, pl.ds(base, 128)] = u
                tab[at, pl.ds(base + HALF, 128)] = v

    loop(0, 16, make_rows)

    own = jnp.broadcast_to(info_ref[:, pl.ds(0, CB)].astype(jnp.float32), (CB, CB))
    diagonal = lax.broadcasted_iota(jnp.int32, (CB, CB), 0) == lax.broadcasted_iota(
        jnp.int32, (CB, CB), 1
    )
    column = jnp.sum(jnp.where(diagonal, own, 0.0), axis=1, keepdims=True)
    valid_ref[...] = jnp.broadcast_to(column, (CB, CB))

    power[:, pl.ds(0, 128)] = jnp.zeros((rows, 128), jnp.bfloat16)
    power[:, pl.ds(128 + NB, 128)] = jnp.zeros((rows, 128), jnp.bfloat16)
    near = (
        lax.broadcasted_iota(jnp.int32, (512, 256), 0)
        - lax.broadcasted_iota(jnp.int32, (512, 256), 1)
        - 128
    )
    band = jnp.where(jnp.abs(near) <= HW, 1.0, 0.0).astype(jnp.bfloat16)

    def exchange(i, r):
        to = peer(me, r)
        return pltpu.make_async_remote_copy(
            send.at[i, to // 2, to % 2],
            recv.at[i, me],
            send_sem.at[i, to],
            recv_sem.at[i, me],
            device_id={"chan": to},
            device_id_type=MESH,
        )

    def arrival(i, r):
        source = peer(me, r)
        return pltpu.make_async_copy(recv.at[i, source], recv.at[i, source], recv_sem.at[i, source])

    def keep(i):
        return pltpu.make_async_copy(send.at[i, me // 2, me % 2], recv.at[i, me], own_sem.at[i])

    def tell(r):
        to = peer(me, r)
        return pltpu.make_async_remote_copy(
            info_ref,
            info.at[me],
            info_send.at[to],
            info_recv.at[me],
            device_id={"chan": to},
            device_id_type=MESH,
        )

    def told(r):
        source = peer(me, r)
        return pltpu.make_async_copy(info.at[source], info.at[source], info_recv.at[source])

    pl.semaphore_wait(barrier, chans - 1 + quarters - 1)

    def whiten_step(i):
        load(i).wait()

        def transform(n):
            cols = pl.ds(pl.multiple_of(n * 256, 256), 256)
            block = x_ref[pl.ds(i * segs, segs)].reshape(rows, NT)
            spec[:, cols] = jnp.dot(block, tab[:, cols], preferred_element_type=jnp.float32)

        loop(0, 2 * NB // 256, transform)

        def add_power(n):
            at = pl.ds(pl.multiple_of(n * 32, 32), 32)
            for chunk in range(NB // 256):
                base = (chunk // 2) * NB + (chunk % 2) * 256
                re, im = spec[at, pl.ds(base, 256)], spec[at, pl.ds(base + HALF, 256)]
                power[at, pl.ds(128 + chunk * 256, 256)] = (re * re + im * im).astype(jnp.bfloat16)

        loop(0, rows // 32, add_power)

        for chunk in range(NB // 256):
            total = jnp.dot(
                power[:, pl.ds(chunk * 256, 512)], band, preferred_element_type=jnp.float32
            )
            k = chunk * 256 + lax.broadcasted_iota(jnp.int32, (1, 256), 1)
            count = jnp.minimum(k + HW, NB - 1) - jnp.maximum(k - HW, 0) + 1
            inv_level[:, pl.ds(chunk * 256, 256)] = lax.rsqrt(
                total * (1.0 / count.astype(jnp.float32)) + EPSILON
            )

        def scale(g):
            valid = valid_ref[pl.ds(pl.multiple_of(g * 8, 8), 8), :]
            for chunk in range(NB // 128):
                h, at = chunk // 4, (chunk % 4) * 128
                res, ims = [], []
                for s in range(segs):
                    row = pl.ds(pl.multiple_of(s * CB + g * 8, 8), 8)
                    weight = inv_level[row, pl.ds(chunk * 128, 128)] * valid
                    res.append(spec[row, pl.ds(h * NB + at, 128)] * weight)
                    ims.append(spec[row, pl.ds(h * NB + HALF + at, 128)] * weight)
                send[i, g, h, :, pl.ds(at, 128)] = jnp.concatenate(res, 0).astype(jnp.bfloat16)
                send[i, g, h, :, pl.ds(HALF + at, 128)] = jnp.concatenate(ims, 0).astype(jnp.bfloat16)

        loop(0, G, scale)
        keep(i).start()
        loop(1, chans, lambda r: exchange(i, r).start())

    loop(0, STEPS, whiten_step)
    loop(1, chans, lambda r: tell(r).start())

    recv[:, pl.ds(chans, R)] = jnp.zeros((STEPS, R, 8 * segs, NB), jnp.bfloat16)
    acc[...] = jnp.zeros_like(acc)
    load_fine().wait()

    def make_inverse(n):
        h, at = n // 8, pl.multiple_of((n % 8) * 16, 16)
        br, bi = fine_ref[0, h, pl.ds(at, 16)], fine_ref[1, h, pl.ds(at, 16)]
        for a in range(16):
            ar, ai = inv_coarse[0, a], inv_coarse[1, a]
            re, im = ar * br - ai * bi, -(ar * bi + ai * br)
            for which, value in enumerate((re, im)):
                at_row = pl.ds(pl.multiple_of(h * 256 + which * 128 + at, 16), 16)
                high = value.astype(jnp.bfloat16)
                inv_hi[at_row, pl.ds(a * 128, 128)] = high
                low = value - high.astype(jnp.float32)
                inv_lo[at_row, pl.ds(a * 128, 128)] = low.astype(jnp.bfloat16)

    loop(0, 16, make_inverse)

    def products(i, chunk, first):
        re_at = pl.ds(pl.multiple_of(chunk * 128, 128), 128)
        im_at = pl.ds(pl.multiple_of(HALF + chunk * 128, 128), 128)
        re = [recv[i, first + j, :, re_at].astype(jnp.float32) for j in range(4 + R)]
        im = [recv[i, first + j, :, im_at].astype(jnp.float32) for j in range(4 + R)]
        for j in range(4):
            for d in range(1, R + 1):
                p = re[j] * re[j + d] + im[j] * im[j + d]
                q = im[j] * re[j + d] - re[j] * im[j + d]
                t = (d - 1) * chans + first + j
                acc[chunk, t, :, pl.ds(0, 128)] += p.reshape(segs, 8, 128).sum(0)
                acc[chunk, t, :, pl.ds(128, 128)] += q.reshape(segs, 8, 128).sum(0)

    def all_here(i):
        loop(1, chans, lambda r: arrival(i, r).wait())
        keep(i).wait()

    def cross_step(i):
        all_here(i)
        loop(0, chans, lambda n: products(i, n % 4, (n // 4) * 4))

    loop(0, STEPS - 1, cross_step)

    info[pl.ds(me, 1)] = info_ref[...].reshape(1, 1, 256)
    info[pl.ds(chans, 8)] = jnp.zeros((8, 1, 256), jnp.int32)
    loop(1, chans, lambda r: told(r).wait())
    group = me // 2
    lanes = lax.broadcasted_iota(jnp.int32, (chans, CB), 1)
    everyone = info[...].reshape(chans + 8, 256).astype(jnp.float32)
    masks, names = everyone[:, :CB], everyone[:chans, CB:]
    picked = []
    for d in range(1, R + 1):
        both = masks[:chans] * masks[d : d + chans]
        count = jnp.sum(jnp.where(lanes // 8 == group, both, 0.0), axis=1, keepdims=True)
        factor = 1.0 / (total_segs * jnp.maximum(count, 1.0))
        scale_ref[pl.ds((d - 1) * chans, chans), :] = jnp.broadcast_to(factor, (chans, 256))
        mine = lanes == (d - 1) * G + group
        name = jnp.sum(jnp.where(mine, names, 0.0), axis=1, keepdims=True)
        bin_of = lax.broadcasted_iota(jnp.int32, (chans, 256), 1).astype(jnp.float32)
        picked.append(jnp.where(jnp.broadcast_to(name, (chans, 256)) == bin_of, 1.0, 0.0))
    onehot[...] = jnp.concatenate(picked, 0).T.astype(jnp.bfloat16)

    all_here(STEPS - 1)

    def hand_over(q):
        to = (seg + q) % quarters
        return pltpu.make_async_remote_copy(
            raw.at[to],
            raw_in.at[seg],
            raw_send.at[to],
            raw_recv.at[seg],
            device_id={"seg": to},
            device_id_type=MESH,
        )

    def finish_quarter(chunk):
        loop(0, chans // 4, lambda n: products(STEPS - 1, chunk, n * 4))

        def reduce_rows(n):
            at = pl.ds(pl.multiple_of(n * 8, 8), 8)
            raw[chunk, at, :] = acc[chunk, at].sum(1)

        loop(0, tiles // 8, reduce_rows)

    def give(q):
        finish_quarter((seg + q) % quarters)
        hand_over(q).start()

    loop(1, quarters, give)
    finish_quarter(seg)

    def got(q):
        source = (seg + q) % quarters
        pltpu.make_async_copy(raw_in.at[source], raw_in.at[source], raw_recv.at[source]).wait()

    loop(1, quarters, got)
    sums = raw[seg]
    for q in range(1, 4):
        sums = sums + raw_in[(seg + q) % quarters]
    sums = sums * scale_ref[...]
    high = sums.astype(jnp.bfloat16)
    low = (sums - high.astype(jnp.float32)).astype(jnp.bfloat16)
    stacked = jnp.dot(onehot[...], high, preferred_element_type=jnp.float32)
    stacked += jnp.dot(onehot[...], low, preferred_element_type=jnp.float32)
    bins[...] = stacked.reshape(chans, BIN_DEV, 256)

    def deliver(r):
        to = peer(me, r)
        return pltpu.make_async_remote_copy(
            bins.at[to],
            bins_in.at[me],
            bins_send.at[to],
            bins_recv.at[me],
            device_id={"chan": to},
            device_id_type=MESH,
        )

    loop(1, chans, lambda r: deliver(r).start())
    bins_in[me] = bins[me]

    def delivered(r):
        source = peer(me, r)
        pltpu.make_async_copy(bins_in.at[source], bins_in.at[source], bins_recv.at[source]).wait()

    loop(1, chans, delivered)
    halves = []
    for h in range(2):
        total = bins_in[h]
        for g in range(1, G):
            total = total + bins_in[2 * g + h]
        halves.append(total)
    spectra = jnp.concatenate(halves, axis=1)
    high = spectra.astype(jnp.bfloat16)
    low = (spectra - high.astype(jnp.float32)).astype(jnp.bfloat16)
    for n in range(NLAG // 512):
        cols = pl.ds(n * 512, 512)
        value = jnp.dot(high, inv_hi[:, cols], preferred_element_type=jnp.float32)
        value += jnp.dot(low, inv_hi[:, cols], preferred_element_type=jnp.float32)
        value += jnp.dot(high, inv_lo[:, cols], preferred_element_type=jnp.float32)
        part[:, cols] = value

    def share(q):
        to = (seg + q) % quarters
        return pltpu.make_async_remote_copy(
            part,
            part_in.at[seg],
            part_send.at[to],
            part_recv.at[seg],
            device_id={"seg": to},
            device_id_type=MESH,
        )

    loop(1, quarters, lambda q: share(q).start())

    def shared(q):
        source = (seg + q) % quarters
        pltpu.make_async_copy(part_in.at[source], part_in.at[source], part_recv.at[source]).wait()

    part_in[seg] = part[...]
    loop(1, quarters, shared)
    out_ref[...] = (part_in[0] + part_in[1]) + (part_in[2] + part_in[3])

    for i in range(STEPS):
        loop(1, chans, lambda r: exchange(i, r).wait_send())
    loop(1, chans, lambda r: tell(r).wait_send())
    loop(1, chans, lambda r: deliver(r).wait_send())
    loop(1, quarters, lambda q: hand_over(q).wait_send())
    loop(1, quarters, lambda q: share(q).wait_send())


def per_device(traces, channel_mask, owner_ids, local_bins):
    chans, quarters = lax.axis_size("chan"), lax.axis_size("seg")
    tiles = chans * R
    segs = traces.shape[0] // STEPS
    labels = owner_ids.reshape(1, -1) * BIN_DEV + local_bins
    info = jnp.concatenate([channel_mask.reshape(1, -1), labels, jnp.zeros_like(labels)], axis=1)
    vmem = pl.BlockSpec(memory_space=pltpu.VMEM)
    anywhere = pl.BlockSpec(memory_space=pl.ANY)
    dma = pltpu.SemaphoreType.DMA
    bf16, f32 = jnp.bfloat16, jnp.float32
    return pl.pallas_call(
        functools.partial(stack_kernel, float(traces.shape[0] * quarters)),
        out_shape=jax.ShapeDtypeStruct((BIN_DEV, NLAG), f32),
        in_specs=[anywhere] + [vmem] * 4 + [anywhere, vmem, vmem],
        out_specs=vmem,
        scratch_shapes=[
            pltpu.VMEM(traces.shape, bf16),
            pltpu.VMEM((NT, 2 * NB), bf16),
            pltpu.VMEM((segs * CB, 2 * NB), f32),
            pltpu.VMEM((segs * CB, NB + 256), bf16),
            pltpu.VMEM((segs * CB, NB), f32),
            pltpu.VMEM((CB, CB), f32),
            pltpu.VMEM((STEPS, G, 2, 8 * segs, NB), bf16),
            pltpu.VMEM((STEPS, chans + R, 8 * segs, NB), bf16),
            pltpu.VMEM((4, tiles, 8, 256), f32),
            pltpu.VMEM((2, 2, 128, 128), f32),
            pltpu.VMEM((512, NLAG), bf16),
            pltpu.VMEM((512, NLAG), bf16),
            pltpu.VMEM((chans + 8, 1, 256), jnp.int32),
            pltpu.VMEM((256, tiles), bf16),
            pltpu.VMEM((tiles, 256), f32),
            pltpu.VMEM((4, tiles, 256), f32),
            pltpu.VMEM((4, tiles, 256), f32),
            pltpu.VMEM((chans, BIN_DEV, 256), f32),
            pltpu.VMEM((chans, BIN_DEV, 256), f32),
            pltpu.VMEM((BIN_DEV, NLAG), f32),
            pltpu.VMEM((4, BIN_DEV, NLAG), f32),
            dma((STEPS,)), dma, dma((STEPS,)), dma((STEPS, chans)), dma((STEPS, chans)),
            dma((chans,)), dma((chans,)), dma((4,)), dma((4,)),
            dma((chans,)), dma((chans,)), dma((4,)), dma((4,)),
        ],
        compiler_params=pltpu.CompilerParams(
            collective_id=0, has_side_effects=True, vmem_limit_bytes=60 << 20
        ),
        name="stack",
    )(traces, *forward_factors(), *inverse_factors(), info)


def solution(mesh):
    in_specs = (P("seg", "chan", None), P("chan"), P("chan", None, None), P("chan", None))
    return jax.shard_map(
        per_device, mesh=mesh, in_specs=in_specs, out_specs=P("chan", None), check_vma=False
    )
```

time: 311 us -> 105 us (0.34)
  blocking collectives: 127 us -> 0 us
  waiting for transfers between devices: 74 us -> 0 us
  Pallas kernels: 77.1 us -> 102 us
  between operations: 14.3 us -> 0.01 us
  matrix products: 4.86 us -> 0 us
  local copies, waits for them, and re-layouts: 6.33 us -> 1.55 us
  starting transfers between devices: 3.91 us -> 0 us
    unnamed x1 -> x0, blocking collectives: 127 us -> none
    psum x1 -> x0, waiting for transfers between devices: 68 us -> none  [per_device(): return lax.psum(lags, 'seg')]
    pallas_call x1, Pallas kernels: 77.1 us -> 102 us  [per_device(): pl.pallas_call(functools.partial(stack_kernel, float(traces.shape[0] * qu...]
    all_to_all x1 -> x0, waiting for transfers between devices: 5.95 us -> none  [per_device(): lax.all_to_all(stacked.reshape(chan_count, BIN_DEV, 256), 'chan', split_a...]
    dot_general x3 -> x0, matrix products: 4.86 us -> none  [the longest x1 2.04 us: per_device(): stacked = jnp.dot(stacker, sums, precision=lax.Precision.HIGHEST)]
    all_to_all x1 -> x0, starting transfers between devices: 3.87 us -> none  [per_device(): lax.all_to_all(stacked.reshape(chan_count, BIN_DEV, 256), 'chan', split_a...]
  transfers between devices with their start and end apart: 3 -> 0, of which waited for: 2 -> 0; matrix products, arithmetic and copies ran while one was open for 2% -> 0% of each run, Pallas kernels for 0% -> 0%
where the time goes in v2:
time: 105 us
  Pallas kernels  102 us (97%)
  other arithmetic  1.9 us (2%)
  local copies, waits for them, and re-layouts  1.55 us (1%)
    pallas_call x1, Pallas kernels, per_device(): pl.pallas_call(functools.partial(stack_kernel, float(traces.shape[0] * qu...  102 us

profile of v2, /device:TPU:1, one launch (start us, length us, event | category | flops | bytes accessed | tf_op | source)
XLA Modules:
  0.0 105.0 jit_solution(3248297675434779948)
XLA Ops:
  0.0 0.7 bitcast_add_fusion
  0.7 0.1 pad.2.clone
  0.8 1.2 %add_add_fusion.info_ref = s32[1,256]{1,0:T(1,128)} fusion(s32[1,256]{1,0:T(1,128)S(1)} %bitcast.4, s32[1,64]{1,0:T(1,128)S(1)} %bitcast_add_fusion, s32[1,128]{1,0:T(1,128)} %bitcast.5), kind=kLoop, calls=%fused_computation | loop fusion | flops 512 | bytes 2816 | tf_op jit(solution)/shard_map/concatenate | solution.py:397
  2.0 101.5 %stack.1 = f32[8,2048]{1,0:T(8,128)} custom-call(bf16[8,128,4096]{2,1,0:T(8,128)(2,1)} %traces.1, f32[16,1,1024]{2,1,0:T(1,128)} %constant.16.clone.coarse_re, f32[16,1,1024]{2,1,0:T(1,128)} %constant.17.clone.coarse_im, f32[64,1024]{1,0:T(8,128)} %constant.18.clone.fine_re, f32[64,1024]{1,0:T(8,128)} %constant.19.clone.fine_im, ...), custom_call_target="tpu_custom_call" | custom-call | tf_op jit(solution)/shard_map/stack/pallas_call | solution.py:402
  103.5 1.5 %copy.12 = f32[8,2048]{1,0:T(8,128)} copy(f32[8,2048]{1,0:T(8,128)} %stack.1) | data formatting | bytes 131072
  (1 shorter events, 0.0 us)

commit v3 on v2

--- a/solution.py
+++ b/solution.py
@@ -62,14 +62,16 @@
     traces, coarse_re, coarse_im, fine_re, fine_im, inv_fine, inv_coarse, info_ref,
     out_ref,
     x_ref, tab, spec, power, inv_level, valid_ref, send, recv, acc,
-    fine_ref, inv_hi, inv_lo, info, onehot, scale_ref, raw, raw_in, bins, bins_in, part, part_in,
-    x_sem, fine_sem, own_sem, send_sem, recv_sem,
-    info_send, info_recv, raw_send, raw_recv, bins_send, bins_recv, part_send, part_recv,
+    fine_ref, inv_hi, inv_lo, info, onehot, scale_ref, raw, raw_in, half, half_in,
+    bins, bins_in, part, part_in,
+    x_sem, fine_sem, own_sem, send_sem, recv_sem, info_send, info_recv, raw_send, raw_recv,
+    half_send, half_recv, bins_send, bins_recv, part_send, part_recv,
 ):
     chans = lax.axis_size("chan")
-    quarters = lax.axis_size("seg")
     me = lax.axis_index("chan")
     seg = lax.axis_index("seg")
+    other_core = seg + 1 - 2 * (seg % 2)
+    other_chip = (seg + 2) % 4
     segs = x_ref.shape[0] // STEPS
     rows = segs * CB
     tiles = chans * R
@@ -90,12 +92,9 @@
     def greet(r):
         pl.semaphore_signal(barrier, inc=1, device_id={"chan": peer(me, r)}, device_id_type=MESH)
 
-    def greet_seg(q):
-        to = (seg + q) % quarters
+    for to in (other_core, other_chip):
         pl.semaphore_signal(barrier, inc=1, device_id={"seg": to}, device_id_type=MESH)
-
     loop(1, chans, greet)
-    loop(1, quarters, greet_seg)
 
     turn = lax.broadcasted_iota(jnp.int32, (64, 128), 1) % 4
     c0 = jnp.where(turn == 0, 1.0, jnp.where(turn == 2, -1.0, 0.0)).astype(jnp.bfloat16)
@@ -139,37 +138,31 @@
     def exchange(i, r):
         to = peer(me, r)
         return pltpu.make_async_remote_copy(
-            send.at[i, to // 2, to % 2],
+            send.at[i, to],
             recv.at[i, me],
-            send_sem.at[i, to],
-            recv_sem.at[i, me],
+            send_sem.at[i],
+            recv_sem.at[i],
             device_id={"chan": to},
             device_id_type=MESH,
         )
 
-    def arrival(i, r):
-        source = peer(me, r)
-        return pltpu.make_async_copy(recv.at[i, source], recv.at[i, source], recv_sem.at[i, source])
+    def await_all(ref, sem):
+        pieces = ref.at[pl.ds(0, chans - 1)]
+        pltpu.make_async_copy(pieces, pieces, sem).wait()
 
     def keep(i):
-        return pltpu.make_async_copy(send.at[i, me // 2, me % 2], recv.at[i, me], own_sem.at[i])
+        return pltpu.make_async_copy(send.at[i, me], recv.at[i, me], own_sem.at[i])
 
     def tell(r):
         to = peer(me, r)
         return pltpu.make_async_remote_copy(
             info_ref,
             info.at[me],
-            info_send.at[to],
-            info_recv.at[me],
+            info_send,
+            info_recv,
             device_id={"chan": to},
             device_id_type=MESH,
         )
-
-    def told(r):
-        source = peer(me, r)
-        return pltpu.make_async_copy(info.at[source], info.at[source], info_recv.at[source])
-
-    pl.semaphore_wait(barrier, chans - 1 + quarters - 1)
 
     def whiten_step(i):
         load(i).wait()
@@ -210,18 +203,26 @@
                     weight = inv_level[row, pl.ds(chunk * 128, 128)] * valid
                     res.append(spec[row, pl.ds(h * NB + at, 128)] * weight)
                     ims.append(spec[row, pl.ds(h * NB + HALF + at, 128)] * weight)
-                send[i, g, h, :, pl.ds(at, 128)] = jnp.concatenate(res, 0).astype(jnp.bfloat16)
-                send[i, g, h, :, pl.ds(HALF + at, 128)] = jnp.concatenate(ims, 0).astype(jnp.bfloat16)
+                send[i, 2 * g + h, :, pl.ds(at, 128)] = jnp.concatenate(res, 0).astype(jnp.bfloat16)
+                send[i, 2 * g + h, :, pl.ds(HALF + at, 128)] = jnp.concatenate(ims, 0).astype(jnp.bfloat16)
 
         loop(0, G, scale)
         keep(i).start()
+
+    def send_step(i):
         loop(1, chans, lambda r: exchange(i, r).start())
 
-    loop(0, STEPS, whiten_step)
+    def later_step(i):
+        whiten_step(i)
+        send_step(i)
+
+    whiten_step(0)
+    pl.semaphore_wait(barrier, chans + 1)
+    send_step(0)
     loop(1, chans, lambda r: tell(r).start())
+    loop(1, STEPS, later_step)
 
     recv[:, pl.ds(chans, R)] = jnp.zeros((STEPS, R, 8 * segs, NB), jnp.bfloat16)
-    acc[...] = jnp.zeros_like(acc)
     load_fine().wait()
 
     def make_inverse(n):
@@ -239,7 +240,7 @@
 
     loop(0, 16, make_inverse)
 
-    def products(i, chunk, first):
+    def products(i, chunk, first, add=True):
         re_at = pl.ds(pl.multiple_of(chunk * 128, 128), 128)
         im_at = pl.ds(pl.multiple_of(HALF + chunk * 128, 128), 128)
         re = [recv[i, first + j, :, re_at].astype(jnp.float32) for j in range(4 + R)]
@@ -249,22 +250,28 @@
                 p = re[j] * re[j + d] + im[j] * im[j + d]
                 q = im[j] * re[j + d] - re[j] * im[j + d]
                 t = (d - 1) * chans + first + j
-                acc[chunk, t, :, pl.ds(0, 128)] += p.reshape(segs, 8, 128).sum(0)
-                acc[chunk, t, :, pl.ds(128, 128)] += q.reshape(segs, 8, 128).sum(0)
+                p, q = p.reshape(segs, 8, 128).sum(0), q.reshape(segs, 8, 128).sum(0)
+                if add:
+                    p = p + acc[chunk, t, :, pl.ds(0, 128)]
+                    q = q + acc[chunk, t, :, pl.ds(128, 128)]
+                acc[chunk, t, :, pl.ds(0, 128)] = p
+                acc[chunk, t, :, pl.ds(128, 128)] = q
 
     def all_here(i):
-        loop(1, chans, lambda r: arrival(i, r).wait())
+        await_all(recv.at[i], recv_sem.at[i])
         keep(i).wait()
 
     def cross_step(i):
         all_here(i)
         loop(0, chans, lambda n: products(i, n % 4, (n // 4) * 4))
 
-    loop(0, STEPS - 1, cross_step)
+    all_here(0)
+    loop(0, chans, lambda n: products(0, n % 4, (n // 4) * 4, add=False))
+    loop(1, STEPS - 1, cross_step)
 
     info[pl.ds(me, 1)] = info_ref[...].reshape(1, 1, 256)
     info[pl.ds(chans, 8)] = jnp.zeros((8, 1, 256), jnp.int32)
-    loop(1, chans, lambda r: told(r).wait())
+    await_all(info, info_recv)
     group = me // 2
     lanes = lax.broadcasted_iota(jnp.int32, (chans, CB), 1)
     everyone = info[...].reshape(chans + 8, 256).astype(jnp.float32)
@@ -283,14 +290,13 @@
 
     all_here(STEPS - 1)
 
-    def hand_over(q):
-        to = (seg + q) % quarters
+    def hand_over(n, chunk):
         return pltpu.make_async_remote_copy(
-            raw.at[to],
-            raw_in.at[seg],
-            raw_send.at[to],
-            raw_recv.at[seg],
-            device_id={"seg": to},
+            raw.at[chunk],
+            raw_in.at[n],
+            raw_send.at[n],
+            raw_recv.at[n],
+            device_id={"seg": other_core},
             device_id_type=MESH,
         )
 
@@ -303,52 +309,52 @@
 
         loop(0, tiles // 8, reduce_rows)
 
-    def give(q):
-        finish_quarter((seg + q) % quarters)
-        hand_over(q).start()
-
-    loop(1, quarters, give)
+    chip = seg - seg % 2
+    far = 2 - chip
+
+    def give(n):
+        chunk = jnp.where(n == 0, far, chip) + other_core % 2
+        finish_quarter(chunk)
+        hand_over(n, chunk).start()
+
+    loop(0, 2, give)
+    cross_chip = pltpu.make_async_remote_copy(
+        half, half_in, half_send, half_recv, device_id={"seg": other_chip}, device_id_type=MESH
+    )
+    finish_quarter(other_chip)
+    hand_over(0, far + other_core % 2).wait()
+    half[...] = (raw[other_chip] + raw_in[0]).astype(jnp.bfloat16)
+    cross_chip.start()
     finish_quarter(seg)
-
-    def got(q):
-        source = (seg + q) % quarters
-        pltpu.make_async_copy(raw_in.at[source], raw_in.at[source], raw_recv.at[source]).wait()
-
-    loop(1, quarters, got)
-    sums = raw[seg]
-    for q in range(1, 4):
-        sums = sums + raw_in[(seg + q) % quarters]
+    hand_over(1, other_core).wait()
+    cross_chip.wait()
+    sums = raw[seg] + raw_in[1] + half_in[...].astype(jnp.float32)
     sums = sums * scale_ref[...]
     high = sums.astype(jnp.bfloat16)
     low = (sums - high.astype(jnp.float32)).astype(jnp.bfloat16)
     stacked = jnp.dot(onehot[...], high, preferred_element_type=jnp.float32)
     stacked += jnp.dot(onehot[...], low, preferred_element_type=jnp.float32)
-    bins[...] = stacked.reshape(chans, BIN_DEV, 256)
+    bins[...] = stacked.reshape(chans, BIN_DEV, 256).astype(jnp.bfloat16)
 
     def deliver(r):
         to = peer(me, r)
         return pltpu.make_async_remote_copy(
             bins.at[to],
             bins_in.at[me],
-            bins_send.at[to],
-            bins_recv.at[me],
+            bins_send,
+            bins_recv,
             device_id={"chan": to},
             device_id_type=MESH,
         )
 
     loop(1, chans, lambda r: deliver(r).start())
     bins_in[me] = bins[me]
-
-    def delivered(r):
-        source = peer(me, r)
-        pltpu.make_async_copy(bins_in.at[source], bins_in.at[source], bins_recv.at[source]).wait()
-
-    loop(1, chans, delivered)
+    await_all(bins_in, bins_recv)
     halves = []
     for h in range(2):
-        total = bins_in[h]
+        total = bins_in[h].astype(jnp.float32)
         for g in range(1, G):
-            total = total + bins_in[2 * g + h]
+            total = total + bins_in[2 * g + h].astype(jnp.float32)
         halves.append(total)
     spectra = jnp.concatenate(halves, axis=1)
     high = spectra.astype(jnp.bfloat16)
@@ -358,35 +364,29 @@
         value = jnp.dot(high, inv_hi[:, cols], preferred_element_type=jnp.float32)
         value += jnp.dot(low, inv_hi[:, cols], preferred_element_type=jnp.float32)
         value += jnp.dot(high, inv_lo[:, cols], preferred_element_type=jnp.float32)
-        part[:, cols] = value
-
-    def share(q):
-        to = (seg + q) % quarters
+        part[0, :, cols] = value
+
+    def share(n, to):
         return pltpu.make_async_remote_copy(
-            part,
-            part_in.at[seg],
-            part_send.at[to],
-            part_recv.at[seg],
+            part.at[n],
+            part_in.at[n],
+            part_send.at[n],
+            part_recv.at[n],
             device_id={"seg": to},
             device_id_type=MESH,
         )
 
-    loop(1, quarters, lambda q: share(q).start())
-
-    def shared(q):
-        source = (seg + q) % quarters
-        pltpu.make_async_copy(part_in.at[source], part_in.at[source], part_recv.at[source]).wait()
-
-    part_in[seg] = part[...]
-    loop(1, quarters, shared)
-    out_ref[...] = (part_in[0] + part_in[1]) + (part_in[2] + part_in[3])
+    share(0, other_core).start()
+    share(0, other_core).wait()
+    part[1] = part[0] + part_in[0]
+    share(1, other_chip).start()
+    share(1, other_chip).wait()
+    out_ref[...] = part[1] + part_in[1]
 
     for i in range(STEPS):
-        loop(1, chans, lambda r: exchange(i, r).wait_send())
-    loop(1, chans, lambda r: tell(r).wait_send())
-    loop(1, chans, lambda r: deliver(r).wait_send())
-    loop(1, quarters, lambda q: hand_over(q).wait_send())
-    loop(1, quarters, lambda q: share(q).wait_send())
+        await_all(send.at[i], send_sem.at[i])
+    await_all(info, info_send)
+    await_all(bins_in, bins_send)
 
 
 def per_device(traces, channel_mask, owner_ids, local_bins):
@@ -411,7 +411,7 @@
             pltpu.VMEM((segs * CB, NB + 256), bf16),
             pltpu.VMEM((segs * CB, NB), f32),
             pltpu.VMEM((CB, CB), f32),
-            pltpu.VMEM((STEPS, G, 2, 8 * segs, NB), bf16),
+            pltpu.VMEM((STEPS, chans, 8 * segs, NB), bf16),
             pltpu.VMEM((STEPS, chans + R, 8 * segs, NB), bf16),
             pltpu.VMEM((4, tiles, 8, 256), f32),
             pltpu.VMEM((2, 2, 128, 128), f32),
@@ -421,14 +421,15 @@
             pltpu.VMEM((256, tiles), bf16),
             pltpu.VMEM((tiles, 256), f32),
             pltpu.VMEM((4, tiles, 256), f32),
-            pltpu.VMEM((4, tiles, 256), f32),
-            pltpu.VMEM((chans, BIN_DEV, 256), f32),
-            pltpu.VMEM((chans, BIN_DEV, 256), f32),
-            pltpu.VMEM((BIN_DEV, NLAG), f32),
-            pltpu.VMEM((4, BIN_DEV, NLAG), f32),
-            dma((STEPS,)), dma, dma((STEPS,)), dma((STEPS, chans)), dma((STEPS, chans)),
-            dma((chans,)), dma((chans,)), dma((4,)), dma((4,)),
-            dma((chans,)), dma((chans,)), dma((4,)), dma((4,)),
+            pltpu.VMEM((2, tiles, 256), f32),
+            pltpu.VMEM((tiles, 256), bf16),
+            pltpu.VMEM((tiles, 256), bf16),
+            pltpu.VMEM((chans, BIN_DEV, 256), bf16),
+            pltpu.VMEM((chans, BIN_DEV, 256), bf16),
+            pltpu.VMEM((2, BIN_DEV, NLAG), f32),
+            pltpu.VMEM((2, BIN_DEV, NLAG), f32),
+            dma((STEPS,)), dma, dma((STEPS,)), dma((STEPS,)), dma((STEPS,)),
+            dma, dma, dma((2,)), dma((2,)), dma, dma, dma, dma, dma((2,)), dma((2,)),
         ],
         compiler_params=pltpu.CompilerParams(
             collective_id=0, has_side_effects=True, vmem_limit_bytes=60 << 20

time: 105 us -> 91.8 us (0.87)
  Pallas kernels: 102 us -> 88.2 us
    pallas_call x1, Pallas kernels: 102 us -> 88.2 us  [per_device(): pl.pallas_call(functools.partial(stack_kernel, float(traces.shape[0] * qu...]
where the time goes in v3:
time: 91.8 us; the launch traced here: 91.6 us
  Pallas kernels  88.2 us (96%)
  other arithmetic  1.9 us (2%)
  local copies, waits for them, and re-layouts  1.55 us (2%)
    pallas_call x1, Pallas kernels, per_device(): pl.pallas_call(functools.partial(stack_kernel, float(traces.shape[0] * qu...  88.2 us

profile of v3, /device:TPU:1, one launch (start us, length us, event | category | flops | bytes accessed | tf_op | source)
XLA Modules:
  0.0 91.6 jit_solution(14743088325652797615)
XLA Ops:
  0.0 0.7 bitcast_add_fusion
  0.7 0.1 pad.2.clone
  0.8 1.2 %add_add_fusion.info_ref = s32[1,256]{1,0:T(1,128)} fusion(s32[1,256]{1,0:T(1,128)S(1)} %bitcast.4, s32[1,64]{1,0:T(1,128)S(1)} %bitcast_add_fusion, s32[1,128]{1,0:T(1,128)} %bitcast.5), kind=kLoop, calls=%fused_computation | loop fusion | flops 512 | bytes 2816 | tf_op jit(solution)/shard_map/concatenate | solution.py:397
  2.0 88.2 %stack.1 = f32[8,2048]{1,0:T(8,128)} custom-call(bf16[8,128,4096]{2,1,0:T(8,128)(2,1)} %traces.1, f32[16,1,1024]{2,1,0:T(1,128)} %constant.16.clone.coarse_re, f32[16,1,1024]{2,1,0:T(1,128)} %constant.17.clone.coarse_im, f32[64,1024]{1,0:T(8,128)} %constant.18.clone.fine_re, f32[64,1024]{1,0:T(8,128)} %constant.19.clone.fine_im, ...), custom_call_target="tpu_custom_call" | custom-call | tf_op jit(solution)/shard_map/stack/pallas_call | solution.py:402
  90.2 1.5 %copy.12 = f32[8,2048]{1,0:T(8,128)} copy(f32[8,2048]{1,0:T(8,128)} %stack.1) | data formatting | bytes 131072
  (1 shorter events, 0.0 us)

commit v4 on v3

--- a/solution.py
+++ b/solution.py
@@ -20,7 +20,7 @@
 NLAG = 2048
 HALF = NB // 2
 EPSILON = 1e-06
-STEPS = 4
+STEPS = ((0, 1), (1, 1), (2, 2), (4, 2), (6, 2))
 MESH = pl.DeviceIdType.MESH
 
 
@@ -59,10 +59,10 @@
 
 def stack_kernel(
     total_segs,
-    traces, coarse_re, coarse_im, fine_re, fine_im, inv_fine, inv_coarse, info_ref,
+    traces, coarse_re, coarse_im, fine_re, fine_im, inv_fine, inv_coarse, mask_row, owners, locals_,
     out_ref,
-    x_ref, tab, spec, power, inv_level, valid_ref, send, recv, acc,
-    fine_ref, inv_hi, inv_lo, info, onehot, scale_ref, raw, raw_in, half, half_in,
+    x_ref, tab, spec, power, inv_level, valid_ref, send_one, recv_one, send_two, recv_two, acc,
+    info_ref, fine_ref, inv_hi, inv_lo, info, onehot, scale_ref, raw, raw_in, half, half_in,
     bins, bins_in, part, part_in,
     x_sem, fine_sem, own_sem, send_sem, recv_sem, info_send, info_recv, raw_send, raw_recv,
     half_send, half_recv, bins_send, bins_recv, part_send, part_recv,
@@ -72,20 +72,21 @@
     seg = lax.axis_index("seg")
     other_core = seg + 1 - 2 * (seg % 2)
     other_chip = (seg + 2) % 4
-    segs = x_ref.shape[0] // STEPS
-    rows = segs * CB
     tiles = chans * R
 
     def load(i):
-        part_of = pl.ds(i * segs, segs)
-        return pltpu.make_async_copy(traces.at[part_of], x_ref.at[part_of], x_sem.at[i])
+        at = pl.ds(*STEPS[i])
+        return pltpu.make_async_copy(traces.at[at], x_ref.at[at], x_sem.at[i])
 
     def load_fine():
         return pltpu.make_async_copy(inv_fine.at[:, :, seg], fine_ref, fine_sem)
 
-    for i in range(STEPS):
+    for i in range(len(STEPS)):
         load(i).start()
     load_fine().start()
+    info_ref[:, pl.ds(0, CB)] = mask_row[...]
+    info_ref[:, pl.ds(CB, CB)] = jnp.zeros((1, CB), jnp.int32)
+    info_ref[:, pl.ds(CB, R * G)] = owners[...] * BIN_DEV + locals_[...]
 
     barrier = pltpu.get_barrier_semaphore()
 
@@ -126,8 +127,8 @@
     column = jnp.sum(jnp.where(diagonal, own, 0.0), axis=1, keepdims=True)
     valid_ref[...] = jnp.broadcast_to(column, (CB, CB))
 
-    power[:, pl.ds(0, 128)] = jnp.zeros((rows, 128), jnp.bfloat16)
-    power[:, pl.ds(128 + NB, 128)] = jnp.zeros((rows, 128), jnp.bfloat16)
+    power[:, pl.ds(0, 128)] = jnp.zeros((2 * CB, 128), jnp.bfloat16)
+    power[:, pl.ds(128 + NB, 128)] = jnp.zeros((2 * CB, 128), jnp.bfloat16)
     near = (
         lax.broadcasted_iota(jnp.int32, (512, 256), 0)
         - lax.broadcasted_iota(jnp.int32, (512, 256), 1)
@@ -135,23 +136,26 @@
     )
     band = jnp.where(jnp.abs(near) <= HW, 1.0, 0.0).astype(jnp.bfloat16)
 
+    send = [send_one.at[0], send_one.at[1]] + [send_two.at[i] for i in range(3)]
+    recv = [recv_one.at[0], recv_one.at[1]] + [recv_two.at[i] for i in range(3)]
+
     def exchange(i, r):
         to = peer(me, r)
         return pltpu.make_async_remote_copy(
-            send.at[i, to],
-            recv.at[i, me],
+            send[i].at[to],
+            recv[i].at[me],
             send_sem.at[i],
             recv_sem.at[i],
             device_id={"chan": to},
             device_id_type=MESH,
         )
 
+    def keep(i):
+        return pltpu.make_async_copy(send[i].at[me], recv[i].at[me], own_sem.at[i])
+
     def await_all(ref, sem):
         pieces = ref.at[pl.ds(0, chans - 1)]
         pltpu.make_async_copy(pieces, pieces, sem).wait()
-
-    def keep(i):
-        return pltpu.make_async_copy(send.at[i, me], recv.at[i, me], own_sem.at[i])
 
     def tell(r):
         to = peer(me, r)
@@ -164,15 +168,22 @@
             device_id_type=MESH,
         )
 
+    def await_step(ref, i, sem):
+        pieces = ref[i].at[pl.ds(0, chans - 1)]
+        pltpu.make_async_copy(pieces, pieces, sem.at[i]).wait()
+
     def whiten_step(i):
+        first, segs = STEPS[i]
+        rows = segs * CB
+        every = pl.ds(0, rows)
         load(i).wait()
 
         def transform(n):
-            cols = pl.ds(pl.multiple_of(n * 256, 256), 256)
-            block = x_ref[pl.ds(i * segs, segs)].reshape(rows, NT)
-            spec[:, cols] = jnp.dot(block, tab[:, cols], preferred_element_type=jnp.float32)
-
-        loop(0, 2 * NB // 256, transform)
+            cols = pl.ds(pl.multiple_of(n * 512, 512), 512)
+            block = x_ref[pl.ds(first, segs)].reshape(rows, NT)
+            spec[every, cols] = jnp.dot(block, tab[:, cols], preferred_element_type=jnp.float32)
+
+        loop(0, 2 * NB // 512, transform)
 
         def add_power(n):
             at = pl.ds(pl.multiple_of(n * 32, 32), 32)
@@ -185,44 +196,45 @@
 
         for chunk in range(NB // 256):
             total = jnp.dot(
-                power[:, pl.ds(chunk * 256, 512)], band, preferred_element_type=jnp.float32
+                power[every, pl.ds(chunk * 256, 512)], band, preferred_element_type=jnp.float32
             )
             k = chunk * 256 + lax.broadcasted_iota(jnp.int32, (1, 256), 1)
             count = jnp.minimum(k + HW, NB - 1) - jnp.maximum(k - HW, 0) + 1
-            inv_level[:, pl.ds(chunk * 256, 256)] = lax.rsqrt(
+            inv_level[every, pl.ds(chunk * 256, 256)] = lax.rsqrt(
                 total * (1.0 / count.astype(jnp.float32)) + EPSILON
             )
 
         def scale(g):
             valid = valid_ref[pl.ds(pl.multiple_of(g * 8, 8), 8), :]
-            for chunk in range(NB // 128):
-                h, at = chunk // 4, (chunk % 4) * 128
-                res, ims = [], []
-                for s in range(segs):
-                    row = pl.ds(pl.multiple_of(s * CB + g * 8, 8), 8)
+            for s in range(segs):
+                row = pl.ds(pl.multiple_of(s * CB + g * 8, 8), 8)
+                for chunk in range(NB // 128):
+                    h, at = chunk // 4, (chunk % 4) * 128
                     weight = inv_level[row, pl.ds(chunk * 128, 128)] * valid
-                    res.append(spec[row, pl.ds(h * NB + at, 128)] * weight)
-                    ims.append(spec[row, pl.ds(h * NB + HALF + at, 128)] * weight)
-                send[i, 2 * g + h, :, pl.ds(at, 128)] = jnp.concatenate(res, 0).astype(jnp.bfloat16)
-                send[i, 2 * g + h, :, pl.ds(HALF + at, 128)] = jnp.concatenate(ims, 0).astype(jnp.bfloat16)
+                    re = spec[row, pl.ds(h * NB + at, 128)] * weight
+                    im = spec[row, pl.ds(h * NB + HALF + at, 128)] * weight
+                    to = 2 * g + h
+                    block = send[i].at[to, s] if segs == 2 else send[i].at[to]
+                    block[:, pl.ds(at, 128)] = re.astype(jnp.bfloat16)
+                    block[:, pl.ds(HALF + at, 128)] = im.astype(jnp.bfloat16)
 
         loop(0, G, scale)
         keep(i).start()
 
     def send_step(i):
-        loop(1, chans, lambda r: exchange(i, r).start())
-
-    def later_step(i):
-        whiten_step(i)
-        send_step(i)
+        loop(1, chans, lambda r: exchange(i, chans - r).start())
 
     whiten_step(0)
     pl.semaphore_wait(barrier, chans + 1)
     send_step(0)
-    loop(1, chans, lambda r: tell(r).start())
-    loop(1, STEPS, later_step)
-
-    recv[:, pl.ds(chans, R)] = jnp.zeros((STEPS, R, 8 * segs, NB), jnp.bfloat16)
+    for i in range(1, len(STEPS)):
+        whiten_step(i)
+        send_step(i)
+        if i == 2:
+            loop(1, chans, lambda r: tell(r).start())
+
+    for block in recv:
+        block[pl.ds(chans, R)] = jnp.zeros((R,) + block.shape[1:], jnp.bfloat16)
     load_fine().wait()
 
     def make_inverse(n):
@@ -240,34 +252,39 @@
 
     loop(0, 16, make_inverse)
 
-    def products(i, chunk, first, add=True):
+    def products(pair, chunk, first, add=True):
         re_at = pl.ds(pl.multiple_of(chunk * 128, 128), 128)
         im_at = pl.ds(pl.multiple_of(HALF + chunk * 128, 128), 128)
-        re = [recv[i, first + j, :, re_at].astype(jnp.float32) for j in range(4 + R)]
-        im = [recv[i, first + j, :, im_at].astype(jnp.float32) for j in range(4 + R)]
+
+        def part_of(j, s, at):
+            block = recv[s].at[first + j] if pair == 0 else recv[pair + 1].at[first + j, s]
+            return block[:, at].astype(jnp.float32)
+
+        re = [[part_of(j, s, re_at) for j in range(4 + R)] for s in range(2)]
+        im = [[part_of(j, s, im_at) for j in range(4 + R)] for s in range(2)]
         for j in range(4):
             for d in range(1, R + 1):
-                p = re[j] * re[j + d] + im[j] * im[j + d]
-                q = im[j] * re[j + d] - re[j] * im[j + d]
                 t = (d - 1) * chans + first + j
-                p, q = p.reshape(segs, 8, 128).sum(0), q.reshape(segs, 8, 128).sum(0)
+                p = re[0][j] * re[0][j + d] + im[0][j] * im[0][j + d]
+                q = im[0][j] * re[0][j + d] - re[0][j] * im[0][j + d]
+                p += re[1][j] * re[1][j + d] + im[1][j] * im[1][j + d]
+                q += im[1][j] * re[1][j + d] - re[1][j] * im[1][j + d]
                 if add:
                     p = p + acc[chunk, t, :, pl.ds(0, 128)]
                     q = q + acc[chunk, t, :, pl.ds(128, 128)]
                 acc[chunk, t, :, pl.ds(0, 128)] = p
                 acc[chunk, t, :, pl.ds(128, 128)] = q
 
-    def all_here(i):
-        await_all(recv.at[i], recv_sem.at[i])
+    def here(i):
+        await_step(recv, i, recv_sem)
         keep(i).wait()
 
-    def cross_step(i):
-        all_here(i)
-        loop(0, chans, lambda n: products(i, n % 4, (n // 4) * 4))
-
-    all_here(0)
+    here(0)
+    here(1)
     loop(0, chans, lambda n: products(0, n % 4, (n // 4) * 4, add=False))
-    loop(1, STEPS - 1, cross_step)
+    for i in (2, 3):
+        here(i)
+        loop(0, chans, lambda n: products(i - 1, n % 4, (n // 4) * 4))
 
     info[pl.ds(me, 1)] = info_ref[...].reshape(1, 1, 256)
     info[pl.ds(chans, 8)] = jnp.zeros((8, 1, 256), jnp.int32)
@@ -288,7 +305,7 @@
         picked.append(jnp.where(jnp.broadcast_to(name, (chans, 256)) == bin_of, 1.0, 0.0))
     onehot[...] = jnp.concatenate(picked, 0).T.astype(jnp.bfloat16)
 
-    all_here(STEPS - 1)
+    here(len(STEPS) - 1)
 
     def hand_over(n, chunk):
         return pltpu.make_async_remote_copy(
@@ -301,7 +318,7 @@
         )
 
     def finish_quarter(chunk):
-        loop(0, chans // 4, lambda n: products(STEPS - 1, chunk, n * 4))
+        loop(0, chans // 4, lambda n: products(3, chunk, n * 4))
 
         def reduce_rows(n):
             at = pl.ds(pl.multiple_of(n * 8, 8), 8)
@@ -347,7 +364,8 @@
             device_id_type=MESH,
         )
 
-    loop(1, chans, lambda r: deliver(r).start())
+    for r in range(1, chans):
+        deliver(r).start()
     bins_in[me] = bins[me]
     await_all(bins_in, bins_recv)
     halves = []
@@ -359,42 +377,44 @@
     spectra = jnp.concatenate(halves, axis=1)
     high = spectra.astype(jnp.bfloat16)
     low = (spectra - high.astype(jnp.float32)).astype(jnp.bfloat16)
-    for n in range(NLAG // 512):
-        cols = pl.ds(n * 512, 512)
-        value = jnp.dot(high, inv_hi[:, cols], preferred_element_type=jnp.float32)
-        value += jnp.dot(low, inv_hi[:, cols], preferred_element_type=jnp.float32)
-        value += jnp.dot(high, inv_lo[:, cols], preferred_element_type=jnp.float32)
-        part[0, :, cols] = value
-
-    def share(n, to):
+    both = jnp.concatenate([high, low], axis=0)
+
+    def share(hop, n, to):
         return pltpu.make_async_remote_copy(
-            part.at[n],
-            part_in.at[n],
-            part_send.at[n],
-            part_recv.at[n],
+            part.at[hop, n],
+            part_in.at[hop, n],
+            part_send.at[hop, n],
+            part_recv.at[hop, n],
             device_id={"seg": to},
             device_id_type=MESH,
         )
 
-    share(0, other_core).start()
-    share(0, other_core).wait()
-    part[1] = part[0] + part_in[0]
-    share(1, other_chip).start()
-    share(1, other_chip).wait()
-    out_ref[...] = part[1] + part_in[1]
-
-    for i in range(STEPS):
-        await_all(send.at[i], send_sem.at[i])
+    chunks = range(NLAG // 512)
+    for n in chunks:
+        at = pl.ds(n * 512, 512)
+        value = jnp.dot(both, inv_hi[:, at], preferred_element_type=jnp.float32)
+        value = value[:BIN_DEV] + value[BIN_DEV:]
+        value += jnp.dot(high, inv_lo[:, at], preferred_element_type=jnp.float32)
+        part[0, n] = value
+        share(0, n, other_core).start()
+    for n in chunks:
+        share(0, n, other_core).wait()
+        part[1, n] = part[0, n] + part_in[0, n]
+        share(1, n, other_chip).start()
+    for n in chunks:
+        at = pl.ds(n * 512, 512)
+        share(1, n, other_chip).wait()
+        out_ref[:, at] = part[1, n] + part_in[1, n]
+
+    for i in range(len(STEPS)):
+        await_step(send, i, send_sem)
     await_all(info, info_send)
     await_all(bins_in, bins_send)
 
 
 def per_device(traces, channel_mask, owner_ids, local_bins):
     chans, quarters = lax.axis_size("chan"), lax.axis_size("seg")
-    tiles = chans * R
-    segs = traces.shape[0] // STEPS
-    labels = owner_ids.reshape(1, -1) * BIN_DEV + local_bins
-    info = jnp.concatenate([channel_mask.reshape(1, -1), labels, jnp.zeros_like(labels)], axis=1)
+    tiles, steps = chans * R, len(STEPS)
     vmem = pl.BlockSpec(memory_space=pltpu.VMEM)
     anywhere = pl.BlockSpec(memory_space=pl.ANY)
     dma = pltpu.SemaphoreType.DMA
@@ -402,18 +422,21 @@
     return pl.pallas_call(
         functools.partial(stack_kernel, float(traces.shape[0] * quarters)),
         out_shape=jax.ShapeDtypeStruct((BIN_DEV, NLAG), f32),
-        in_specs=[anywhere] + [vmem] * 4 + [anywhere, vmem, vmem],
+        in_specs=[anywhere] + [vmem] * 4 + [anywhere] + [vmem] * 4,
         out_specs=vmem,
         scratch_shapes=[
             pltpu.VMEM(traces.shape, bf16),
             pltpu.VMEM((NT, 2 * NB), bf16),
-            pltpu.VMEM((segs * CB, 2 * NB), f32),
-            pltpu.VMEM((segs * CB, NB + 256), bf16),
-            pltpu.VMEM((segs * CB, NB), f32),
+            pltpu.VMEM((2 * CB, 2 * NB), f32),
+            pltpu.VMEM((2 * CB, NB + 256), bf16),
+            pltpu.VMEM((2 * CB, NB), f32),
             pltpu.VMEM((CB, CB), f32),
-            pltpu.VMEM((STEPS, chans, 8 * segs, NB), bf16),
-            pltpu.VMEM((STEPS, chans + R, 8 * segs, NB), bf16),
+            pltpu.VMEM((2, chans, 8, NB), bf16),
+            pltpu.VMEM((2, chans + R, 8, NB), bf16),
+            pltpu.VMEM((3, chans, 2, 8, NB), bf16),
+            pltpu.VMEM((3, chans + R, 2, 8, NB), bf16),
             pltpu.VMEM((4, tiles, 8, 256), f32),
+            pltpu.VMEM((1, 2 * CB), jnp.int32),
             pltpu.VMEM((2, 2, 128, 128), f32),
             pltpu.VMEM((512, NLAG), bf16),
             pltpu.VMEM((512, NLAG), bf16),
@@ -426,16 +449,23 @@
             pltpu.VMEM((tiles, 256), bf16),
             pltpu.VMEM((chans, BIN_DEV, 256), bf16),
             pltpu.VMEM((chans, BIN_DEV, 256), bf16),
-            pltpu.VMEM((2, BIN_DEV, NLAG), f32),
-            pltpu.VMEM((2, BIN_DEV, NLAG), f32),
-            dma((STEPS,)), dma, dma((STEPS,)), dma((STEPS,)), dma((STEPS,)),
-            dma, dma, dma((2,)), dma((2,)), dma, dma, dma, dma, dma((2,)), dma((2,)),
+            pltpu.VMEM((2, 4, BIN_DEV, NLAG // 4), f32),
+            pltpu.VMEM((2, 4, BIN_DEV, NLAG // 4), f32),
+            dma((steps,)), dma, dma((steps,)), dma((steps,)), dma((steps,)),
+            dma, dma, dma((2,)), dma((2,)), dma, dma, dma, dma, dma((2, 4)), dma((2, 4)),
         ],
         compiler_params=pltpu.CompilerParams(
             collective_id=0, has_side_effects=True, vmem_limit_bytes=60 << 20
         ),
         name="stack",
-    )(traces, *forward_factors(), *inverse_factors(), info)
+    )(
+        traces,
+        *forward_factors(),
+        *inverse_factors(),
+        channel_mask.reshape(1, -1),
+        owner_ids.reshape(1, -1),
+        local_bins,
+    )
 
 
 def solution(mesh):

time: 91.8 us -> 85.5 us (0.931)
  Pallas kernels: 88.2 us -> 83.8 us
  other arithmetic: 1.9 us -> 0 us
    pallas_call x1, Pallas kernels: 88.2 us -> 83.8 us  [per_device(): pl.pallas_call(functools.partial(stack_kernel, float(traces.shape[0] * qu...]
    concatenate x1 -> x0, other arithmetic: 1.22 us -> none  [per_device(): jnp.concatenate([channel_mask.reshape(1, -1), labels, jnp.zeros_like(labe...]
where the time goes in v4:
time: 85.5 us; the launch traced here: 85.3 us
  Pallas kernels  83.8 us (98%)
  local copies, waits for them, and re-layouts  1.47 us (2%)
    pallas_call x1, Pallas kernels, per_device(): pl.pallas_call(functools.partial(stack_kernel, float(traces.shape[0] * qu...  83.8 us

profile of v4, /device:TPU:1, one launch (start us, length us, event | category | flops | bytes accessed | tf_op | source)
XLA Modules:
  0.0 85.3 jit_solution(5784248803478546369)
XLA Ops:
  0.0 83.8 %stack.1 = f32[8,2048]{1,0:T(8,128)} custom-call(bf16[8,128,4096]{2,1,0:T(8,128)(2,1)} %traces.1, f32[16,1,1024]{2,1,0:T(1,128)} %constant.12.clone.coarse_re, f32[16,1,1024]{2,1,0:T(1,128)} %constant.13.clone.coarse_im, f32[64,1024]{1,0:T(8,128)} %constant.14.clone.fine_re, f32[64,1024]{1,0:T(8,128)} %constant.15.clone.fine_im, ...), custom_call_target="tpu_custom_call" | custom-call | tf_op jit(solution)/shard_map/stack/pallas_call | solution.py:422
  83.9 1.5 %copy.12 = f32[8,2048]{1,0:T(8,128)} copy(f32[8,2048]{1,0:T(8,128)} %stack.1) | data formatting | bytes 131072

commit v5 on v4

--- a/solution.py
+++ b/solution.py
@@ -19,6 +19,7 @@
 NB = 1024
 NLAG = 2048
 HALF = NB // 2
+QUARTER = NT // 4
 EPSILON = 1e-06
 STEPS = ((0, 1), (1, 1), (2, 2), (4, 2), (6, 2))
 MESH = pl.DeviceIdType.MESH
@@ -61,7 +62,7 @@
     total_segs,
     traces, coarse_re, coarse_im, fine_re, fine_im, inv_fine, inv_coarse, mask_row, owners, locals_,
     out_ref,
-    x_ref, tab, spec, power, inv_level, valid_ref, send_one, recv_one, send_two, recv_two, acc,
+    x_ref, tab, parts, spec, power, inv_level, valid_ref, send_one, recv_one, send_two, recv_two, acc,
     info_ref, fine_ref, inv_hi, inv_lo, info, onehot, scale_ref, raw, raw_in, half, half_in,
     bins, bins_in, part, part_in,
     x_sem, fine_sem, own_sem, send_sem, recv_sem, info_send, info_recv, raw_send, raw_recv,
@@ -76,13 +77,19 @@
 
     def load(i):
         at = pl.ds(*STEPS[i])
-        return pltpu.make_async_copy(traces.at[at], x_ref.at[at], x_sem.at[i])
+        return [
+            pltpu.make_async_copy(
+                traces.at[at, :, pl.ds(q * QUARTER, QUARTER)], x_ref.at[at, q], x_sem.at[i, q]
+            )
+            for q in range(4)
+        ]
 
     def load_fine():
         return pltpu.make_async_copy(inv_fine.at[:, :, seg], fine_ref, fine_sem)
 
     for i in range(len(STEPS)):
-        load(i).start()
+        for copy in load(i):
+            copy.start()
     load_fine().start()
     info_ref[:, pl.ds(0, CB)] = mask_row[...]
     info_ref[:, pl.ds(CB, CB)] = jnp.zeros((1, CB), jnp.int32)
@@ -97,28 +104,22 @@
         pl.semaphore_signal(barrier, inc=1, device_id={"seg": to}, device_id_type=MESH)
     loop(1, chans, greet)
 
-    turn = lax.broadcasted_iota(jnp.int32, (64, 128), 1) % 4
-    c0 = jnp.where(turn == 0, 1.0, jnp.where(turn == 2, -1.0, 0.0)).astype(jnp.bfloat16)
-    c1 = jnp.where(turn == 1, 1.0, jnp.where(turn == 3, -1.0, 0.0)).astype(jnp.bfloat16)
-    flip = jnp.where(turn % 2 == 0, 1.0, -1.0).astype(jnp.bfloat16)
-
     def make_rows(a):
+        at = pl.ds(pl.multiple_of(a * 64, 64), 64)
         for chunk in range(NB // 128):
             cols = pl.ds(chunk * 128, 128)
             ar, ai = coarse_re[a, :, cols], coarse_im[a, :, cols]
             br, bi = fine_re[:, cols], fine_im[:, cols]
-            re = (ar * br - ai * bi).astype(jnp.bfloat16)
-            im = (ar * bi + ai * br).astype(jnp.bfloat16)
-            re1, im1 = re * c0 + im * c1, im * c0 - re * c1
             base = (chunk // 4) * NB + (chunk % 4) * 128
-            for quarter, (u, v) in enumerate(
-                ((re, im), (re1, im1), (re * flip, im * flip), (re1 * flip, im1 * flip))
-            ):
-                at = pl.ds(pl.multiple_of(quarter * 1024 + a * 64, 64), 64)
-                tab[at, pl.ds(base, 128)] = u
-                tab[at, pl.ds(base + HALF, 128)] = v
-
-    loop(0, 16, make_rows)
+            tab[at, pl.ds(base, 128)] = (ar * br - ai * bi).astype(jnp.bfloat16)
+            tab[at, pl.ds(base + HALF, 128)] = (ar * bi + ai * br).astype(jnp.bfloat16)
+
+    loop(0, QUARTER // 64, make_rows)
+
+    turn = lax.broadcasted_iota(jnp.int32, (16, 256), 1) % 4
+    c0 = jnp.where(turn == 0, 1.0, jnp.where(turn == 2, -1.0, 0.0))
+    c1 = jnp.where(turn == 1, 1.0, jnp.where(turn == 3, -1.0, 0.0))
+    flip = jnp.where(turn % 2 == 0, 1.0, -1.0)
 
     own = jnp.broadcast_to(info_ref[:, pl.ds(0, CB)].astype(jnp.float32), (CB, CB))
     diagonal = lax.broadcasted_iota(jnp.int32, (CB, CB), 0) == lax.broadcasted_iota(
@@ -176,23 +177,36 @@
         first, segs = STEPS[i]
         rows = segs * CB
         every = pl.ds(0, rows)
-        load(i).wait()
+        for copy in load(i):
+            copy.wait()
 
         def transform(n):
             cols = pl.ds(pl.multiple_of(n * 512, 512), 512)
-            block = x_ref[pl.ds(first, segs)].reshape(rows, NT)
-            spec[every, cols] = jnp.dot(block, tab[:, cols], preferred_element_type=jnp.float32)
+            block = x_ref[pl.ds(first, segs)].reshape(4 * rows, QUARTER)
+            parts[pl.ds(0, 4 * rows), cols] = jnp.dot(
+                block, tab[:, cols], preferred_element_type=jnp.float32
+            )
 
         loop(0, 2 * NB // 512, transform)
 
         def add_power(n):
-            at = pl.ds(pl.multiple_of(n * 32, 32), 32)
+            at = pl.ds(pl.multiple_of(n * 16, 16), 16)
+            s, row = n // (CB // 16), n % (CB // 16)
             for chunk in range(NB // 256):
                 base = (chunk // 2) * NB + (chunk % 2) * 256
-                re, im = spec[at, pl.ds(base, 256)], spec[at, pl.ds(base + HALF, 256)]
+                res, ims = [], []
+                for q in range(4):
+                    rows_of = pl.ds(pl.multiple_of((s * 4 + q) * CB + row * 16, 16), 16)
+                    res.append(parts[rows_of, pl.ds(base, 256)])
+                    ims.append(parts[rows_of, pl.ds(base + HALF, 256)])
+                b_re, b_im = res[1] + flip * res[3], ims[1] + flip * ims[3]
+                re = res[0] + flip * res[2] + (c0 * b_re + c1 * b_im)
+                im = ims[0] + flip * ims[2] + (c0 * b_im - c1 * b_re)
+                spec[at, pl.ds(base, 256)] = re
+                spec[at, pl.ds(base + HALF, 256)] = im
                 power[at, pl.ds(128 + chunk * 256, 256)] = (re * re + im * im).astype(jnp.bfloat16)
 
-        loop(0, rows // 32, add_power)
+        loop(0, rows // 16, add_power)
 
         for chunk in range(NB // 256):
             total = jnp.dot(
@@ -379,33 +393,36 @@
     low = (spectra - high.astype(jnp.float32)).astype(jnp.bfloat16)
     both = jnp.concatenate([high, low], axis=0)
 
-    def share(hop, n, to):
+    def share(n, q):
         return pltpu.make_async_remote_copy(
-            part.at[hop, n],
-            part_in.at[hop, n],
-            part_send.at[hop, n],
-            part_recv.at[hop, n],
-            device_id={"seg": to},
+            part.at[n],
+            part_in.at[n, seg],
+            part_send.at[n, q],
+            part_recv.at[n, seg],
+            device_id={"seg": (seg + q) % 4},
             device_id_type=MESH,
         )
 
-    chunks = range(NLAG // 512)
-    for n in chunks:
-        at = pl.ds(n * 512, 512)
+    width = NLAG // 2
+    for n in range(2):
+        at = pl.ds(n * width, width)
         value = jnp.dot(both, inv_hi[:, at], preferred_element_type=jnp.float32)
         value = value[:BIN_DEV] + value[BIN_DEV:]
         value += jnp.dot(high, inv_lo[:, at], preferred_element_type=jnp.float32)
-        part[0, n] = value
-        share(0, n, other_core).start()
-    for n in chunks:
-        share(0, n, other_core).wait()
-        part[1, n] = part[0, n] + part_in[0, n]
-        share(1, n, other_chip).start()
-    for n in chunks:
-        at = pl.ds(n * 512, 512)
-        share(1, n, other_chip).wait()
-        out_ref[:, at] = part[1, n] + part_in[1, n]
-
+        part[n] = value.astype(jnp.bfloat16)
+        for q in (2, 1, 3):
+            share(n, q).start()
+        part_in[n, seg] = value.astype(jnp.bfloat16)
+    for n in range(2):
+        for q in (1, 2, 3):
+            source = part_in.at[n, (seg + q) % 4]
+            pltpu.make_async_copy(source, source, part_recv.at[n, (seg + q) % 4]).wait()
+        terms = [part_in[n, q].astype(jnp.float32) for q in range(4)]
+        out_ref[:, pl.ds(n * width, width)] = (terms[0] + terms[1]) + (terms[2] + terms[3])
+
+    for n in range(2):
+        for q in (1, 2, 3):
+            share(n, q).wait_send()
     for i in range(len(STEPS)):
         await_step(send, i, send_sem)
     await_all(info, info_send)
@@ -425,8 +442,9 @@
         in_specs=[anywhere] + [vmem] * 4 + [anywhere] + [vmem] * 4,
         out_specs=vmem,
         scratch_shapes=[
-            pltpu.VMEM(traces.shape, bf16),
-            pltpu.VMEM((NT, 2 * NB), bf16),
+            pltpu.VMEM((traces.shape[0], 4, CB, QUARTER), bf16),
+            pltpu.VMEM((QUARTER, 2 * NB), bf16),
+            pltpu.VMEM((8 * CB, 2 * NB), f32),
             pltpu.VMEM((2 * CB, 2 * NB), f32),
             pltpu.VMEM((2 * CB, NB + 256), bf16),
             pltpu.VMEM((2 * CB, NB), f32),
@@ -449,9 +467,9 @@
             pltpu.VMEM((tiles, 256), bf16),
             pltpu.VMEM((chans, BIN_DEV, 256), bf16),
             pltpu.VMEM((chans, BIN_DEV, 256), bf16),
-            pltpu.VMEM((2, 4, BIN_DEV, NLAG // 4), f32),
-            pltpu.VMEM((2, 4, BIN_DEV, NLAG // 4), f32),
-            dma((steps,)), dma, dma((steps,)), dma((steps,)), dma((steps,)),
+            pltpu.VMEM((2, BIN_DEV, NLAG // 2), bf16),
+            pltpu.VMEM((2, 4, BIN_DEV, NLAG // 2), bf16),
+            dma((steps, 4)), dma, dma((steps,)), dma((steps,)), dma((steps,)),
             dma, dma, dma((2,)), dma((2,)), dma, dma, dma, dma, dma((2, 4)), dma((2, 4)),
         ],
         compiler_params=pltpu.CompilerParams(

time: 85.5 us -> 82.5 us (0.965)
  Pallas kernels: 83.8 us -> 80.8 us
    pallas_call x1, Pallas kernels: 83.8 us -> 80.8 us  [per_device(): pl.pallas_call(functools.partial(stack_kernel, float(traces.shape[0] * qu...]
where the time goes in v5:
time: 82.5 us; the launch traced here: 82.3 us
  Pallas kernels  80.8 us (98%)
  local copies, waits for them, and re-layouts  1.47 us (2%)
    pallas_call x1, Pallas kernels, per_device(): pl.pallas_call(functools.partial(stack_kernel, float(traces.shape[0] * qu...  80.8 us

profile of v5, /device:TPU:1, one launch (start us, length us, event | category | flops | bytes accessed | tf_op | source)
XLA Modules:
  0.0 82.3 jit_solution(2276641210342495926)
XLA Ops:
  0.0 80.8 %stack.1 = f32[8,2048]{1,0:T(8,128)} custom-call(bf16[8,128,4096]{2,1,0:T(8,128)(2,1)} %traces.1, f32[16,1,1024]{2,1,0:T(1,128)} %constant.12.clone.coarse_re, f32[16,1,1024]{2,1,0:T(1,128)} %constant.13.clone.coarse_im, f32[64,1024]{1,0:T(8,128)} %constant.14.clone.fine_re, f32[64,1024]{1,0:T(8,128)} %constant.15.clone.fine_im, ...), custom_call_target="tpu_custom_call" | custom-call | tf_op jit(solution)/shard_map/stack/pallas_call | solution.py:439
  80.8 1.5 %copy.12 = f32[8,2048]{1,0:T(8,128)} copy(f32[8,2048]{1,0:T(8,128)} %stack.1) | data formatting | bytes 131072

commit v6 on v5

--- a/solution.py
+++ b/solution.py
@@ -21,7 +21,7 @@
 HALF = NB // 2
 QUARTER = NT // 4
 EPSILON = 1e-06
-STEPS = ((0, 1), (1, 1), (2, 2), (4, 2), (6, 2))
+STEPS = ((0, 1), (1, 1), (2, 2), (4, 2), (6, 1), (7, 1))
 MESH = pl.DeviceIdType.MESH
 
 
@@ -60,13 +60,12 @@
 
 def stack_kernel(
     total_segs,
-    traces, coarse_re, coarse_im, fine_re, fine_im, inv_fine, inv_coarse, mask_row, owners, locals_,
+    traces, coarse_re, coarse_im, fine_re, fine_im, inv_fine, inv_coarse_hbm, mask_row, owners, locals_,
     out_ref,
     x_ref, tab, parts, spec, power, inv_level, valid_ref, send_one, recv_one, send_two, recv_two, acc,
-    info_ref, fine_ref, inv_hi, inv_lo, info, onehot, scale_ref, raw, raw_in, half, half_in,
-    bins, bins_in, part, part_in,
+    info_ref, fine_ref, inv_coarse, inv_hi, inv_lo, info, onehot, scale_ref, raw, raw_in, bins, bins_in, part, part_in,
     x_sem, fine_sem, own_sem, send_sem, recv_sem, info_send, info_recv, raw_send, raw_recv,
-    half_send, half_recv, bins_send, bins_recv, part_send, part_recv,
+    bins_send, bins_recv, part_send, part_recv, entered,
 ):
     chans = lax.axis_size("chan")
     me = lax.axis_index("chan")
@@ -85,12 +84,16 @@
         ]
 
     def load_fine():
-        return pltpu.make_async_copy(inv_fine.at[:, :, seg], fine_ref, fine_sem)
+        return (
+            pltpu.make_async_copy(inv_fine.at[:, :, seg], fine_ref, fine_sem.at[0]),
+            pltpu.make_async_copy(inv_coarse_hbm, inv_coarse, fine_sem.at[1]),
+        )
 
     for i in range(len(STEPS)):
         for copy in load(i):
             copy.start()
-    load_fine().start()
+    for copy in load_fine():
+        copy.start()
     info_ref[:, pl.ds(0, CB)] = mask_row[...]
     info_ref[:, pl.ds(CB, CB)] = jnp.zeros((1, CB), jnp.int32)
     info_ref[:, pl.ds(CB, R * G)] = owners[...] * BIN_DEV + locals_[...]
@@ -102,9 +105,9 @@
 
     for to in (other_core, other_chip):
         pl.semaphore_signal(barrier, inc=1, device_id={"seg": to}, device_id_type=MESH)
-    loop(1, chans, greet)
 
     def make_rows(a):
+        greet(2 * a + 1)
         at = pl.ds(pl.multiple_of(a * 64, 64), 64)
         for chunk in range(NB // 128):
             cols = pl.ds(chunk * 128, 128)
@@ -114,7 +117,12 @@
             tab[at, pl.ds(base, 128)] = (ar * br - ai * bi).astype(jnp.bfloat16)
             tab[at, pl.ds(base + HALF, 128)] = (ar * bi + ai * br).astype(jnp.bfloat16)
 
-    loop(0, QUARTER // 64, make_rows)
+    def make_rows_and_greet(a):
+        greet(2 * a + 2)
+        make_rows(a)
+
+    loop(0, chans // 2 - 1, make_rows_and_greet)
+    make_rows(chans // 2 - 1)
 
     turn = lax.broadcasted_iota(jnp.int32, (16, 256), 1) % 4
     c0 = jnp.where(turn == 0, 1.0, jnp.where(turn == 2, -1.0, 0.0))
@@ -137,8 +145,8 @@
     )
     band = jnp.where(jnp.abs(near) <= HW, 1.0, 0.0).astype(jnp.bfloat16)
 
-    send = [send_one.at[0], send_one.at[1]] + [send_two.at[i] for i in range(3)]
-    recv = [recv_one.at[0], recv_one.at[1]] + [recv_two.at[i] for i in range(3)]
+    send = [send_one.at[0], send_one.at[1], send_two.at[0], send_two.at[1], send_one.at[2], send_one.at[3]]
+    recv = [recv_one.at[0], recv_one.at[1], recv_two.at[0], recv_two.at[1], recv_one.at[2], recv_one.at[3]]
 
     def exchange(i, r):
         to = peer(me, r)
@@ -240,6 +248,7 @@
 
     whiten_step(0)
     pl.semaphore_wait(barrier, chans + 1)
+    pl.semaphore_signal(entered, inc=1, device_id={"seg": other_chip}, device_id_type=MESH)
     send_step(0)
     for i in range(1, len(STEPS)):
         whiten_step(i)
@@ -249,7 +258,8 @@
 
     for block in recv:
         block[pl.ds(chans, R)] = jnp.zeros((R,) + block.shape[1:], jnp.bfloat16)
-    load_fine().wait()
+    for copy in load_fine():
+        copy.wait()
 
     def make_inverse(n):
         h, at = n // 8, pl.multiple_of((n % 8) * 16, 16)
@@ -266,26 +276,27 @@
 
     loop(0, 16, make_inverse)
 
-    def products(pair, chunk, first, add=True):
+    def products(steps, chunk, first, add=True):
         re_at = pl.ds(pl.multiple_of(chunk * 128, 128), 128)
         im_at = pl.ds(pl.multiple_of(HALF + chunk * 128, 128), 128)
-
-        def part_of(j, s, at):
-            block = recv[s].at[first + j] if pair == 0 else recv[pair + 1].at[first + j, s]
-            return block[:, at].astype(jnp.float32)
-
-        re = [[part_of(j, s, re_at) for j in range(4 + R)] for s in range(2)]
-        im = [[part_of(j, s, im_at) for j in range(4 + R)] for s in range(2)]
+        blocks = []
+        for i in steps:
+            two = STEPS[i][1] == 2
+            for s in range(STEPS[i][1]):
+                blocks.append(
+                    [recv[i].at[first + j, s] if two else recv[i].at[first + j] for j in range(4 + R)]
+                )
+        re = [[ref[:, re_at].astype(jnp.float32) for ref in refs] for refs in blocks]
+        im = [[ref[:, im_at].astype(jnp.float32) for ref in refs] for refs in blocks]
         for j in range(4):
             for d in range(1, R + 1):
                 t = (d - 1) * chans + first + j
-                p = re[0][j] * re[0][j + d] + im[0][j] * im[0][j + d]
-                q = im[0][j] * re[0][j + d] - re[0][j] * im[0][j + d]
-                p += re[1][j] * re[1][j + d] + im[1][j] * im[1][j + d]
-                q += im[1][j] * re[1][j + d] - re[1][j] * im[1][j + d]
-                if add:
-                    p = p + acc[chunk, t, :, pl.ds(0, 128)]
-                    q = q + acc[chunk, t, :, pl.ds(128, 128)]
+                p, q = (0.0, 0.0) if not add else (
+                    acc[chunk, t, :, pl.ds(0, 128)], acc[chunk, t, :, pl.ds(128, 128)]
+                )
+                for s in range(len(blocks)):
+                    p = p + (re[s][j] * re[s][j + d] + im[s][j] * im[s][j + d])
+                    q = q + (im[s][j] * re[s][j + d] - re[s][j] * im[s][j + d])
                 acc[chunk, t, :, pl.ds(0, 128)] = p
                 acc[chunk, t, :, pl.ds(128, 128)] = q
 
@@ -295,10 +306,10 @@
 
     here(0)
     here(1)
-    loop(0, chans, lambda n: products(0, n % 4, (n // 4) * 4, add=False))
-    for i in (2, 3):
+    loop(0, chans, lambda n: products((0, 1), n % 4, (n // 4) * 4, add=False))
+    for i in (2, 3, 4):
         here(i)
-        loop(0, chans, lambda n: products(i - 1, n % 4, (n // 4) * 4))
+        loop(0, chans, lambda n: products((i,), n % 4, (n // 4) * 4))
 
     info[pl.ds(me, 1)] = info_ref[...].reshape(1, 1, 256)
     info[pl.ds(chans, 8)] = jnp.zeros((8, 1, 256), jnp.int32)
@@ -332,7 +343,7 @@
         )
 
     def finish_quarter(chunk):
-        loop(0, chans // 4, lambda n: products(3, chunk, n * 4))
+        loop(0, chans // 4, lambda n: products((len(STEPS) - 1,), chunk, n * 4))
 
         def reduce_rows(n):
             at = pl.ds(pl.multiple_of(n * 8, 8), 8)
@@ -343,49 +354,47 @@
     chip = seg - seg % 2
     far = 2 - chip
 
-    def give(n):
-        chunk = jnp.where(n == 0, far, chip) + other_core % 2
+    def give(n, chunk):
         finish_quarter(chunk)
         hand_over(n, chunk).start()
 
-    loop(0, 2, give)
-    cross_chip = pltpu.make_async_remote_copy(
-        half, half_in, half_send, half_recv, device_id={"seg": other_chip}, device_id_type=MESH
-    )
+    def stack(n, sums):
+        sums = sums * scale_ref[...]
+        high = sums.astype(jnp.bfloat16)
+        low = (sums - high.astype(jnp.float32)).astype(jnp.bfloat16)
+        stacked = jnp.dot(onehot[...], high, preferred_element_type=jnp.float32)
+        stacked += jnp.dot(onehot[...], low, preferred_element_type=jnp.float32)
+        bins[n] = stacked.reshape(chans, BIN_DEV, 256).astype(jnp.bfloat16)
+
+    def deliver(n, r):
+        to = peer(me, r)
+        return pltpu.make_async_remote_copy(
+            bins.at[n, to],
+            bins_in.at[n * chans + me],
+            bins_send,
+            bins_recv,
+            device_id={"seg": other_chip if n else seg, "chan": to},
+            device_id_type=MESH,
+        )
+
+    give(0, far + other_core % 2)
     finish_quarter(other_chip)
+    give(1, other_core)
     hand_over(0, far + other_core % 2).wait()
-    half[...] = (raw[other_chip] + raw_in[0]).astype(jnp.bfloat16)
-    cross_chip.start()
+    stack(1, raw[other_chip] + raw_in[0])
+    pl.semaphore_wait(entered, 1)
+    loop(0, chans, lambda r: deliver(1, chans - 1 - r).start())
     finish_quarter(seg)
     hand_over(1, other_core).wait()
-    cross_chip.wait()
-    sums = raw[seg] + raw_in[1] + half_in[...].astype(jnp.float32)
-    sums = sums * scale_ref[...]
-    high = sums.astype(jnp.bfloat16)
-    low = (sums - high.astype(jnp.float32)).astype(jnp.bfloat16)
-    stacked = jnp.dot(onehot[...], high, preferred_element_type=jnp.float32)
-    stacked += jnp.dot(onehot[...], low, preferred_element_type=jnp.float32)
-    bins[...] = stacked.reshape(chans, BIN_DEV, 256).astype(jnp.bfloat16)
-
-    def deliver(r):
-        to = peer(me, r)
-        return pltpu.make_async_remote_copy(
-            bins.at[to],
-            bins_in.at[me],
-            bins_send,
-            bins_recv,
-            device_id={"chan": to},
-            device_id_type=MESH,
-        )
-
-    for r in range(1, chans):
-        deliver(r).start()
-    bins_in[me] = bins[me]
-    await_all(bins_in, bins_recv)
+    stack(0, raw[seg] + raw_in[1])
+    loop(1, chans, lambda r: deliver(0, chans - r).start())
+    bins_in[me] = bins[0, me]
+    pieces = bins_in.at[pl.ds(0, 2 * chans - 1)]
+    pltpu.make_async_copy(pieces, pieces, bins_recv).wait()
     halves = []
     for h in range(2):
         total = bins_in[h].astype(jnp.float32)
-        for g in range(1, G):
+        for g in range(1, 2 * G):
             total = total + bins_in[2 * g + h].astype(jnp.float32)
         halves.append(total)
     spectra = jnp.concatenate(halves, axis=1)
@@ -426,7 +435,7 @@
     for i in range(len(STEPS)):
         await_step(send, i, send_sem)
     await_all(info, info_send)
-    await_all(bins_in, bins_send)
+    pltpu.make_async_copy(pieces, pieces, bins_send).wait()
 
 
 def per_device(traces, channel_mask, owner_ids, local_bins):
@@ -439,7 +448,7 @@
     return pl.pallas_call(
         functools.partial(stack_kernel, float(traces.shape[0] * quarters)),
         out_shape=jax.ShapeDtypeStruct((BIN_DEV, NLAG), f32),
-        in_specs=[anywhere] + [vmem] * 4 + [anywhere] + [vmem] * 4,
+        in_specs=[anywhere] + [vmem] * 4 + [anywhere] * 2 + [vmem] * 3,
         out_specs=vmem,
         scratch_shapes=[
             pltpu.VMEM((traces.shape[0], 4, CB, QUARTER), bf16),
@@ -449,13 +458,14 @@
             pltpu.VMEM((2 * CB, NB + 256), bf16),
             pltpu.VMEM((2 * CB, NB), f32),
             pltpu.VMEM((CB, CB), f32),
-            pltpu.VMEM((2, chans, 8, NB), bf16),
-            pltpu.VMEM((2, chans + R, 8, NB), bf16),
-            pltpu.VMEM((3, chans, 2, 8, NB), bf16),
-            pltpu.VMEM((3, chans + R, 2, 8, NB), bf16),
+            pltpu.VMEM((4, chans, 8, NB), bf16),
+            pltpu.VMEM((4, chans + R, 8, NB), bf16),
+            pltpu.VMEM((2, chans, 2, 8, NB), bf16),
+            pltpu.VMEM((2, chans + R, 2, 8, NB), bf16),
             pltpu.VMEM((4, tiles, 8, 256), f32),
             pltpu.VMEM((1, 2 * CB), jnp.int32),
             pltpu.VMEM((2, 2, 128, 128), f32),
+            pltpu.VMEM((2, 16, 16, 128), f32),
             pltpu.VMEM((512, NLAG), bf16),
             pltpu.VMEM((512, NLAG), bf16),
             pltpu.VMEM((chans + 8, 1, 256), jnp.int32),
@@ -463,14 +473,13 @@
             pltpu.VMEM((tiles, 256), f32),
             pltpu.VMEM((4, tiles, 256), f32),
             pltpu.VMEM((2, tiles, 256), f32),
-            pltpu.VMEM((tiles, 256), bf16),
-            pltpu.VMEM((tiles, 256), bf16),
-            pltpu.VMEM((chans, BIN_DEV, 256), bf16),
-            pltpu.VMEM((chans, BIN_DEV, 256), bf16),
+            pltpu.VMEM((2, chans, BIN_DEV, 256), bf16),
+            pltpu.VMEM((2 * chans, BIN_DEV, 256), bf16),
             pltpu.VMEM((2, BIN_DEV, NLAG // 2), bf16),
             pltpu.VMEM((2, 4, BIN_DEV, NLAG // 2), bf16),
-            dma((steps, 4)), dma, dma((steps,)), dma((steps,)), dma((steps,)),
-            dma, dma, dma((2,)), dma((2,)), dma, dma, dma, dma, dma((2, 4)), dma((2, 4)),
+            dma((steps, 4)), dma((2,)), dma((steps,)), dma((steps,)), dma((steps,)),
+            dma, dma, dma((2,)), dma((2,)), dma, dma, dma((2, 4)), dma((2, 4)),
+            pltpu.SemaphoreType.REGULAR,
         ],
         compiler_params=pltpu.CompilerParams(
             collective_id=0, has_side_effects=True, vmem_limit_bytes=60 << 20

time: 82.5 us -> 80.5 us (0.976)
  Pallas kernels: 80.8 us -> 78.9 us
    pallas_call x1, Pallas kernels: 80.8 us -> 78.9 us  [per_device(): pl.pallas_call(functools.partial(stack_kernel, float(traces.shape[0] * qu...]
where the time goes in v6:
time: 80.5 us; the launch traced here: 80.3 us
  Pallas kernels  78.9 us (98%)
  local copies, waits for them, and re-layouts  1.47 us (2%)
    pallas_call x1, Pallas kernels, per_device(): pl.pallas_call(functools.partial(stack_kernel, float(traces.shape[0] * qu...  78.9 us

profile of v6, /device:TPU:1, one launch (start us, length us, event | category | flops | bytes accessed | tf_op | source)
XLA Modules:
  0.0 80.3 jit_solution(15511679035481400275)
XLA Ops:
  0.0 78.9 %stack.1 = f32[8,2048]{1,0:T(8,128)} custom-call(bf16[8,128,4096]{2,1,0:T(8,128)(2,1)} %traces.1, f32[16,1,1024]{2,1,0:T(1,128)} %constant.12.clone.coarse_re, f32[16,1,1024]{2,1,0:T(1,128)} %constant.13.clone.coarse_im, f32[64,1024]{1,0:T(8,128)} %constant.14.clone.fine_re, f32[64,1024]{1,0:T(8,128)} %constant.15.clone.fine_im, ...), custom_call_target="tpu_custom_call" | custom-call | tf_op jit(solution)/shard_map/stack/pallas_call | solution.py:448
  78.9 1.5 %copy.12 = f32[8,2048]{1,0:T(8,128)} copy(f32[8,2048]{1,0:T(8,128)} %stack.1) | data formatting | bytes 131072

commit v7 on v6

--- a/solution.py
+++ b/solution.py
@@ -62,11 +62,12 @@
     total_segs,
     traces, coarse_re, coarse_im, fine_re, fine_im, inv_fine, inv_coarse_hbm, mask_row, owners, locals_,
     out_ref,
-    x_ref, tab, parts, spec, power, inv_level, valid_ref, send_one, recv_one, send_two, recv_two, acc,
+    x_ref, tab_0, tab_1, tab_2, tab_3, parts, spec, power, inv_level, valid_ref, send_one, recv_one, send_two, recv_two, acc,
     info_ref, fine_ref, inv_coarse, inv_hi, inv_lo, info, onehot, scale_ref, raw, raw_in, bins, bins_in, part, part_in,
     x_sem, fine_sem, own_sem, send_sem, recv_sem, info_send, info_recv, raw_send, raw_recv,
     bins_send, bins_recv, part_send, part_recv, entered,
 ):
+    tab = (tab_0, tab_1, tab_2, tab_3)
     chans = lax.axis_size("chan")
     me = lax.axis_index("chan")
     seg = lax.axis_index("seg")
@@ -89,10 +90,7 @@
             pltpu.make_async_copy(inv_coarse_hbm, inv_coarse, fine_sem.at[1]),
         )
 
-    for i in range(len(STEPS)):
-        for copy in load(i):
-            copy.start()
-    for copy in load_fine():
+    for copy in load(0):
         copy.start()
     info_ref[:, pl.ds(0, CB)] = mask_row[...]
     info_ref[:, pl.ds(CB, CB)] = jnp.zeros((1, CB), jnp.int32)
@@ -106,23 +104,26 @@
     for to in (other_core, other_chip):
         pl.semaphore_signal(barrier, inc=1, device_id={"seg": to}, device_id_type=MESH)
 
-    def make_rows(a):
-        greet(2 * a + 1)
-        at = pl.ds(pl.multiple_of(a * 64, 64), 64)
-        for chunk in range(NB // 128):
+    def make_rows(a, half):
+        at = pl.ds(a * 64 if isinstance(a, int) else pl.multiple_of(a * 64, 64), 64)
+        for chunk in range(4 * half, 4 * half + 4):
             cols = pl.ds(chunk * 128, 128)
             ar, ai = coarse_re[a, :, cols], coarse_im[a, :, cols]
             br, bi = fine_re[:, cols], fine_im[:, cols]
-            base = (chunk // 4) * NB + (chunk % 4) * 128
-            tab[at, pl.ds(base, 128)] = (ar * br - ai * bi).astype(jnp.bfloat16)
-            tab[at, pl.ds(base + HALF, 128)] = (ar * bi + ai * br).astype(jnp.bfloat16)
-
-    def make_rows_and_greet(a):
+            base = (chunk % 4) * 128
+            tab[2 * half][at, pl.ds(base, 128)] = (ar * br - ai * bi).astype(jnp.bfloat16)
+            tab[2 * half + 1][at, pl.ds(base, 128)] = (ar * bi + ai * br).astype(jnp.bfloat16)
+
+    def first_half(a):
+        greet(2 * a + 1)
+        make_rows(a, 0)
+
+    def first_half_and_greet(a):
         greet(2 * a + 2)
-        make_rows(a)
-
-    loop(0, chans // 2 - 1, make_rows_and_greet)
-    make_rows(chans // 2 - 1)
+        first_half(a)
+
+    loop(0, chans // 2 - 1, first_half_and_greet)
+    first_half(chans // 2 - 1)
 
     turn = lax.broadcasted_iota(jnp.int32, (16, 256), 1) % 4
     c0 = jnp.where(turn == 0, 1.0, jnp.where(turn == 2, -1.0, 0.0))
@@ -187,15 +188,23 @@
         every = pl.ds(0, rows)
         for copy in load(i):
             copy.wait()
+        if i == 0:
+            for copy in [copy for j in range(1, len(STEPS)) for copy in load(j)]:
+                copy.start()
+            for copy in load_fine():
+                copy.start()
 
         def transform(n):
-            cols = pl.ds(pl.multiple_of(n * 512, 512), 512)
             block = x_ref[pl.ds(first, segs)].reshape(4 * rows, QUARTER)
-            parts[pl.ds(0, 4 * rows), cols] = jnp.dot(
-                block, tab[:, cols], preferred_element_type=jnp.float32
+            parts[pl.ds(0, 4 * rows), pl.ds(n * 512, 512)] = jnp.dot(
+                block, tab[n][...], preferred_element_type=jnp.float32
             )
 
-        loop(0, 2 * NB // 512, transform)
+        for n in range(4):
+            transform(n)
+            if i == 0 and n < 2:
+                for a in range(8 * n, 8 * n + 8):
+                    make_rows(a, 1)
 
         def add_power(n):
             at = pl.ds(pl.multiple_of(n * 16, 16), 16)
@@ -452,7 +461,7 @@
         out_specs=vmem,
         scratch_shapes=[
             pltpu.VMEM((traces.shape[0], 4, CB, QUARTER), bf16),
-            pltpu.VMEM((QUARTER, 2 * NB), bf16),
+            *[pltpu.VMEM((QUARTER, 512), bf16)] * 4,
             pltpu.VMEM((8 * CB, 2 * NB), f32),
             pltpu.VMEM((2 * CB, 2 * NB), f32),
             pltpu.VMEM((2 * CB, NB + 256), bf16),

time: 80.5 us -> 78.9 us (0.980)
  Pallas kernels: 78.9 us -> 77.3 us
    pallas_call x1, Pallas kernels: 78.9 us -> 77.3 us  [per_device(): pl.pallas_call(functools.partial(stack_kernel, float(traces.shape[0] * qu...]
where the time goes in v7:
time: 78.9 us; the launch traced here: 78.8 us
  Pallas kernels  77.3 us (98%)
  local copies, waits for them, and re-layouts  1.47 us (2%)
    pallas_call x1, Pallas kernels, per_device(): pl.pallas_call(functools.partial(stack_kernel, float(traces.shape[0] * qu...  77.3 us

profile of v7, /device:TPU:1, one launch (start us, length us, event | category | flops | bytes accessed | tf_op | source)
XLA Modules:
  0.0 78.8 jit_solution(11236614455443733522)
XLA Ops:
  0.0 77.3 %stack.1 = f32[8,2048]{1,0:T(8,128)} custom-call(bf16[8,128,4096]{2,1,0:T(8,128)(2,1)} %traces.1, f32[16,1,1024]{2,1,0:T(1,128)} %constant.12.clone.coarse_re, f32[16,1,1024]{2,1,0:T(1,128)} %constant.13.clone.coarse_im, f32[64,1024]{1,0:T(8,128)} %constant.14.clone.fine_re, f32[64,1024]{1,0:T(8,128)} %constant.15.clone.fine_im, ...), custom_call_target="tpu_custom_call" | custom-call | tf_op jit(solution)/shard_map/stack/pallas_call | solution.py:457
  77.3 1.5 %copy.12 = f32[8,2048]{1,0:T(8,128)} copy(f32[8,2048]{1,0:T(8,128)} %stack.1) | data formatting | bytes 131072

commit v8 on v7

--- a/solution.py
+++ b/solution.py
@@ -104,6 +104,9 @@
     for to in (other_core, other_chip):
         pl.semaphore_signal(barrier, inc=1, device_id={"seg": to}, device_id_type=MESH)
 
+    for distance in range(1, chans):
+        greet(distance)
+
     def make_rows(a, half):
         at = pl.ds(a * 64 if isinstance(a, int) else pl.multiple_of(a * 64, 64), 64)
         for chunk in range(4 * half, 4 * half + 4):
@@ -114,16 +117,7 @@
             tab[2 * half][at, pl.ds(base, 128)] = (ar * br - ai * bi).astype(jnp.bfloat16)
             tab[2 * half + 1][at, pl.ds(base, 128)] = (ar * bi + ai * br).astype(jnp.bfloat16)
 
-    def first_half(a):
-        greet(2 * a + 1)
-        make_rows(a, 0)
-
-    def first_half_and_greet(a):
-        greet(2 * a + 2)
-        first_half(a)
-
-    loop(0, chans // 2 - 1, first_half_and_greet)
-    first_half(chans // 2 - 1)
+    loop(0, QUARTER // 64, lambda a: make_rows(a, 0))
 
     turn = lax.broadcasted_iota(jnp.int32, (16, 256), 1) % 4
     c0 = jnp.where(turn == 0, 1.0, jnp.where(turn == 2, -1.0, 0.0))

time: 78.9 us -> 78 us (0.989)
  Pallas kernels: 77.3 us -> 76.4 us
    pallas_call x1, Pallas kernels: 77.3 us -> 76.4 us  [per_device(): pl.pallas_call(functools.partial(stack_kernel, float(traces.shape[0] * qu...]
where the time goes in v8:
time: 78 us; the launch traced here: 77.9 us
  Pallas kernels  76.4 us (98%)
  local copies, waits for them, and re-layouts  1.47 us (2%)
    pallas_call x1, Pallas kernels, per_device(): pl.pallas_call(functools.partial(stack_kernel, float(traces.shape[0] * qu...  76.4 us

profile of v8, /device:TPU:1, one launch (start us, length us, event | category | flops | bytes accessed | tf_op | source)
XLA Modules:
  0.0 77.9 jit_solution(3670034332727039671)
XLA Ops:
  0.0 76.4 %stack.1 = f32[8,2048]{1,0:T(8,128)} custom-call(bf16[8,128,4096]{2,1,0:T(8,128)(2,1)} %traces.1, f32[16,1,1024]{2,1,0:T(1,128)} %constant.12.clone.coarse_re, f32[16,1,1024]{2,1,0:T(1,128)} %constant.13.clone.coarse_im, f32[64,1024]{1,0:T(8,128)} %constant.14.clone.fine_re, f32[64,1024]{1,0:T(8,128)} %constant.15.clone.fine_im, ...), custom_call_target="tpu_custom_call" | custom-call | tf_op jit(solution)/shard_map/stack/pallas_call | solution.py:451
  76.4 1.5 %copy.12 = f32[8,2048]{1,0:T(8,128)} copy(f32[8,2048]{1,0:T(8,128)} %stack.1) | data formatting | bytes 131072

commit v9 on v8

--- a/solution.py
+++ b/solution.py
@@ -92,20 +92,24 @@
 
     for copy in load(0):
         copy.start()
+
+    barrier = pltpu.get_barrier_semaphore()
+
+    def greet(r):
+        pl.semaphore_signal(barrier, inc=1, device_id={"chan": peer(me, r)}, device_id_type=MESH)
+
+
+    def hops(n):
+        return min(n % 4, 4 - n % 4) + min(n // 4 % 4, 4 - n // 4 % 4) + n // 16
+
+    for distance in sorted(range(1, chans), key=hops, reverse=True):
+        greet(distance)
+    for to in (other_core, other_chip):
+        pl.semaphore_signal(barrier, inc=1, device_id={"seg": to}, device_id_type=MESH)
+
     info_ref[:, pl.ds(0, CB)] = mask_row[...]
     info_ref[:, pl.ds(CB, CB)] = jnp.zeros((1, CB), jnp.int32)
     info_ref[:, pl.ds(CB, R * G)] = owners[...] * BIN_DEV + locals_[...]
-
-    barrier = pltpu.get_barrier_semaphore()
-
-    def greet(r):
-        pl.semaphore_signal(barrier, inc=1, device_id={"chan": peer(me, r)}, device_id_type=MESH)
-
-    for to in (other_core, other_chip):
-        pl.semaphore_signal(barrier, inc=1, device_id={"seg": to}, device_id_type=MESH)
-
-    for distance in range(1, chans):
-        greet(distance)
 
     def make_rows(a, half):
         at = pl.ds(a * 64 if isinstance(a, int) else pl.multiple_of(a * 64, 64), 64)

time: 78 us -> 78.1 us (level)
  no operation moved by 1% of the time
where the time goes in v9:
time: 78.1 us; the launch traced here: 77.9 us
  Pallas kernels  76.4 us (98%)
  local copies, waits for them, and re-layouts  1.47 us (2%)
    pallas_call x1, Pallas kernels, per_device(): pl.pallas_call(functools.partial(stack_kernel, float(traces.shape[0] * qu...  76.4 us

profile of v9, /device:TPU:1, one launch (start us, length us, event | category | flops | bytes accessed | tf_op | source)
XLA Modules:
  0.0 77.9 jit_solution(7855274701060282650)
XLA Ops:
  0.0 76.4 %stack.1 = f32[8,2048]{1,0:T(8,128)} custom-call(bf16[8,128,4096]{2,1,0:T(8,128)(2,1)} %traces.1, f32[16,1,1024]{2,1,0:T(1,128)} %constant.12.clone.coarse_re, f32[16,1,1024]{2,1,0:T(1,128)} %constant.13.clone.coarse_im, f32[64,1024]{1,0:T(8,128)} %constant.14.clone.fine_re, f32[64,1024]{1,0:T(8,128)} %constant.15.clone.fine_im, ...), custom_call_target="tpu_custom_call" | custom-call | tf_op jit(solution)/shard_map/stack/pallas_call | solution.py:455
  76.4 1.5 %copy.12 = f32[8,2048]{1,0:T(8,128)} copy(f32[8,2048]{1,0:T(8,128)} %stack.1) | data formatting | bytes 131072
